TPU v7x, 32 devices: a whole 2x2x4 slice. The times are simulated.
32 devices in a mesh: dp: 8 (over y, x, core), seq: 4 (over z).
Axes of the slice: x: 2, y: 2, z: 4, core: 2. Of those that a mesh axis runs over, the one named last changes fastest.
Arguments:
- enc_states: bfloat16 [8, 256, 4096], P('dp'), may hold values from -6 to 6
- lengths: int32 [8], replicated, may hold values from 1 to 128, as said below
- prompt_owner_sample: int32 [8], replicated, may hold values from 0 to 7, each once
- t5_gain: float32 [4096], replicated, may hold values from 0.5 to 1.5
- t5_in_weight: bfloat16 [2, 4096, 5120], P(None, None, 'seq'), may hold values from -0.09375 to 0.09375
- t5_out_weight: bfloat16 [5120, 4096], P('seq'), may hold values from -0.078125 to 0.078125
- t5_final_gain: float32 [4096], replicated, may hold values from 0.5 to 1.5
- context_weight: bfloat16 [4096, 3072], P('seq', 'dp'), may hold values from -0.09375 to 0.09375
- text_shift: float32 [8, 3072], P('dp'), may hold values from -3 to 3
- text_scale: float32 [8, 3072], P('dp'), may hold values from -0.5 to 0.5
- kv_weight: bfloat16 [3072, 2, 3072], P('dp', None, 'seq'), may hold values from -0.109375 to 0.109375
- text_key_gain: float32 [128], replicated, may hold values from 0.25 to 1.75
- image_query_key_value: bfloat16 [8, 512, 3, 3072], P('dp', 'seq'), may hold values from -6 to 6
- image_qk_gain: float32 [2, 128], replicated, may hold values from 0.25 to 1.75
- proj_weight: bfloat16 [3072, 3072], P('seq', 'dp'), may hold values from -0.109375 to 0.109375
- dora_a: float32 [3072, 64], P('seq'), may hold values from -0.109375 to 0.109375
- dora_b: float32 [64, 3072], P(None, 'dp'), may hold values from -0.375 to 0.375
- magnitude: float32 [3072], P('dp'), may hold values from 0.5 to 2
- grad_out: bfloat16 [8, 512, 3072], P('dp', 'seq'), may hold values from -6 to 6
Outputs:
- image_out: bfloat16 [8, 512, 3072], P('dp', 'seq')
- grad_a: float32 [3072, 64], P('seq')
- grad_b: float32 [64, 3072], P(None, 'dp')
- grad_magnitude: float32 [3072], P('dp')
Inputs may be any that keep to these rules, and one draw needn't show every extreme that they name: `lengths`: prompt token counts; in every draw one prompt has exactly 128 tokens. `prompt_owner_sample`: each DiT sample index appears exactly once.
All inputs are finite; a program needn't handle non-finite values.
Results may differ from a plain program's by a relative error of at most 0.024.
Values may be sent and summed in bfloat16 or wider, within the bound.
A program may use at most 128 MiB of HBM per device.

v0:
```python
import math

import jax
import jax.numpy as jnp
from jax import lax
from jax.experimental import pallas as pl
from jax.experimental.pallas import tpu as pltpu
from jax.sharding import PartitionSpec as P

HD = 128
MAX_PROMPT = 128
EPSILON = 1e-06


def rms_scale(values, gain):
    return values * lax.rsqrt(jnp.mean(values * values, -1, keepdims=True) + EPSILON) * gain


def attention_kernel(length_ref, text_gain_ref, image_gain_ref, text_key_ref, text_value_ref, image_ref, out_ref):
    def stacked(kind):
        return jnp.concatenate([image_ref[k, kind] for k in range(image_ref.shape[0])], 0)

    queries = rms_scale(stacked(0).astype(jnp.float32), image_gain_ref[0:1, :])
    queries = (queries).astype(jnp.bfloat16)
    key_image = rms_scale(stacked(1).astype(jnp.float32), image_gain_ref[1:2, :]).astype(jnp.bfloat16)
    key_text = rms_scale(text_key_ref[...], text_gain_ref[...]).astype(jnp.bfloat16)
    scale = 1.0 / math.sqrt(HD)
    dims = (((1,), (1,)), ((), ()))
    text_scores = lax.dot_general(queries, key_text, dims, preferred_element_type=jnp.float32) * scale
    image_scores = lax.dot_general(queries, key_image, dims, preferred_element_type=jnp.float32) * scale
    position = lax.broadcasted_iota(jnp.int32, text_scores.shape, 1)
    text_weight = jnp.where(position < length_ref[0], jnp.exp(text_scores), 0.0)
    image_weight = jnp.exp(image_scores)
    denominator = jnp.sum(text_weight, -1, keepdims=True) + jnp.sum(image_weight, -1, keepdims=True)
    mixture = jnp.dot(
        text_weight.astype(jnp.bfloat16),
        text_value_ref[...].astype(jnp.bfloat16),
        preferred_element_type=jnp.float32,
    )
    mixture = mixture + jnp.dot(
        image_weight.astype(jnp.bfloat16), stacked(2), preferred_element_type=jnp.float32
    )
    out_ref[...] = (mixture / denominator).astype(jnp.bfloat16)


def attention(length, text_gain, image_gain, key_value, image_all):
    blocks, kinds, rows, width = image_all.shape
    heads = width // HD
    text = key_value.shape[0]
    vmem = lambda shape, index: pl.BlockSpec(shape, index)
    return pl.pallas_call(
        attention_kernel,
        grid=(heads,),
        out_shape=jax.ShapeDtypeStruct((blocks * rows, width), jnp.bfloat16),
        in_specs=[
            pl.BlockSpec(memory_space=pltpu.SMEM),
            vmem((1, HD), lambda h: (0, 0)),
            vmem((2, HD), lambda h: (0, 0)),
            vmem((text, HD), lambda h: (0, h)),
            vmem((text, HD), lambda h: (0, heads + h)),
            vmem((blocks, kinds, rows, HD), lambda h: (0, 0, 0, h)),
        ],
        out_specs=vmem((blocks * rows, HD), lambda h: (0, h)),
        cost_estimate=pl.CostEstimate(
            flops=4 * heads * blocks * rows * (blocks * rows + text) * HD,
            bytes_accessed=8 * blocks * rows * width,
            transcendentals=heads * blocks * rows * (blocks * rows + text),
        ),
    )(length.reshape(1), text_gain.reshape(1, HD), image_gain, key_value, key_value, image_all)


def peers(axis):
    size, rank = lax.axis_size(axis), lax.axis_index(axis)
    return [(k, lax.rem(rank + k, size)) for k in range(1, size)]


def greet(*axes):
    barrier = pltpu.get_barrier_semaphore()
    count = 0
    for axis in axes:
        for _, peer in peers(axis):
            pl.semaphore_signal(
                barrier, inc=1, device_id={axis: peer}, device_id_type=pl.DeviceIdType.MESH
            )
            count += 1
    pl.semaphore_wait(barrier, count)


def send(source, target, send_sem, recv_sem, axis, peer):
    copy = pltpu.make_async_remote_copy(
        src_ref=source,
        dst_ref=target,
        send_sem=send_sem,
        recv_sem=recv_sem,
        device_id={axis: peer},
        device_id_type=pl.DeviceIdType.MESH,
    )
    copy.start()
    return copy


def finish(copies):
    for copy in copies:
        copy.wait()


def sems(count):
    return [pltpu.SemaphoreType.DMA((count,)), pltpu.SemaphoreType.DMA((count,))]


VMEM = pl.BlockSpec(memory_space=pltpu.VMEM)
SMEM = pl.BlockSpec(memory_space=pltpu.SMEM)


def params(collective_id):
    return pltpu.CompilerParams(
        collective_id=collective_id, has_side_effects=True, vmem_limit_bytes=40 * 2**20
    )


MESH = pl.DeviceIdType.MESH


class Wires:
    def __init__(self, send_sems, recv_sems):
        self.send_sems, self.recv_sems, self.copies = send_sems, recv_sems, []

    def send(self, source, target, axis, peer):
        index = len(self.copies)
        copy = pltpu.make_async_remote_copy(
            src_ref=source,
            dst_ref=target,
            send_sem=self.send_sems.at[index],
            recv_sem=self.recv_sems.at[index],
            device_id={axis: peer},
            device_id_type=MESH,
        )
        copy.start()
        self.copies.append(copy)
        return copy

    def drain(self):
        for copy in self.copies:
            copy.wait_send()


class Place:
    def __init__(self):
        self.pairs = lax.axis_size("dp") // 4
        index = lax.axis_index("dp")
        self.index = index
        self.core = lax.rem(index, 2)
        self.low = lax.rem(lax.div(index, 2), 2)
        self.high = lax.div(index, 4)

    def at(self, step=0, other_low=False, other_core=False):
        high = lax.rem(self.high + step + self.pairs, self.pairs) if step else self.high
        low = 1 - self.low if other_low else self.low
        core = 1 - self.core if other_core else self.core
        return (high * 2 + low) * 2 + core


class Gather:
    def __init__(self, wires, place, own, full, view):
        self.wires, self.place, self.own, self.full, self.view = wires, place, own, full, view
        self.sibling = place.at(other_core=True)
        self.late = []

    def share(self, owner, half=None):
        where = self.view(self.full, owner, half)
        self.late.append(self.wires.send(where, where, "dp", self.sibling))

    def first(self):
        place = self.place
        mine = self.view(self.full, place.index, None)
        send = self.wires.send
        self.low = send(self.own, mine, "dp", place.at(other_low=True))
        self.high = [send(self.own, mine, "dp", place.at(j)) for j in range(1, place.pairs)]
        self.late.append(send(self.own, mine, "dp", self.sibling))

    def second(self):
        place = self.place
        send = self.wires.send
        self.relayed = []
        self.low.wait_recv()
        owner = place.at(other_low=True)
        for j in range(1, place.pairs):
            where = self.view(self.full, owner, 0)
            self.relayed.append((j, 0, send(where, where, "dp", place.at(j))))
        self.share(owner)
        for j in range(1, place.pairs):
            self.high[j - 1].wait_recv()
            owner = place.at(-j)
            where = self.view(self.full, owner, 1)
            self.relayed.append((j, 1, send(where, where, "dp", place.at(other_low=True))))
            self.share(owner)

    def third(self):
        for j, half, copy in self.relayed:
            copy.wait_recv()
            self.share(self.place.at(-j, other_low=True), half)

    def done(self):
        for copy in self.late:
            copy.wait_recv()


def by_rows(rows):
    def view(full, owner, half):
        start, size = owner * rows, rows
        if half is not None:
            size = rows // 2
            start = start + half * size
        return full.at[pl.ds(pl.multiple_of(start, 16), size)]

    return view


def by_columns(rows, width, flat):
    def view(full, owner, half):
        part = pl.ds(0, rows) if half is None else pl.ds(half * (rows // 2), rows // 2)
        if flat:
            return full.at[part, pl.ds(pl.multiple_of(owner * width, 128), width)]
        return full.at[owner, part]

    return view


def flat_columns(width):
    return width % 128 == 0


def column_shape(devices, rows, width):
    return (rows, devices * width) if flat_columns(width) else (devices, rows, width)


def tile_of(width, largest):
    return next(t for t in (largest, largest // 2, 256, 128, width) if width % t == 0)


def front_kernel(
    owner_ref, enc_ref, gain_ref, in_ref, out_ref, final_ref, context_ref, kv_ref, image_ref,
    proj_ref, down_ref, up_ref, magnitude_ref, scale_ref, shift_ref,
    image_all, key_value, gathered, ratio_ref,
    tokens, normed, in_tiles, out_all, hidden, part, sum_slots, encoded, context_all, kv_all,
    context_part, row_slots, stage, prompts, sibling_prompts, final, text_all,
    direction, squares, square_slots, own_scaled,
    in_sems, local_sems, send_sems, recv_sems,
):
    f32, bf16 = jnp.float32, jnp.bfloat16
    count, devices = lax.axis_size("seq"), lax.axis_size("dp")
    rank, data_rank = lax.axis_index("seq"), lax.axis_index("dp")
    place = Place()
    wires = Wires(send_sems, recv_sems)
    text, width_enc = tokens.shape
    feat = encoded.shape[1]
    width = context_part.shape[1]
    rows = stage.shape[0]
    slots, _, _, tile = in_tiles.shape
    tiles = hidden.shape[1] // tile
    depth, own_cols = proj_ref.shape
    flat = flat_columns(own_cols)
    late = count // 2

    def in_copy(i, slot):
        return pltpu.make_async_copy(
            in_ref.at[:, :, pl.ds(pl.multiple_of(i * tile, 128), tile)], in_tiles.at[slot], in_sems.at[slot]
        )

    def local(source, target, index):
        return pltpu.make_async_copy(source, target, local_sems.at[index])

    token_copy = local(enc_ref.at[0, pl.ds(0, text)], tokens, 0)
    token_copy.start()
    for i in range(min(slots, tiles)):
        in_copy(i, i).start()
    out_copy = local(out_ref, out_all, 1)
    out_copy.start()

    def heads_of(owner):
        head_width = image_all.shape[3]
        return pl.ds(pl.multiple_of(owner * head_width, 128), head_width)

    context_view = by_columns(context_ref.shape[0], own_cols, flat)
    scaled_view = by_columns(own_scaled.shape[0], own_cols, flat)
    kv_view = by_rows(kv_ref.shape[0])
    context_gather = Gather(wires, place, context_ref, context_all, context_view)
    kv_gather = Gather(wires, place, kv_ref, kv_all, kv_view)
    scaled_gather = Gather(wires, place, own_scaled, gathered, scaled_view)

    locals_ = [
        local(image_ref.at[:, :, heads_of(rank)], image_all.at[0], 2),
        local(context_ref, context_view(context_all, data_rank, None), 3),
        local(kv_ref, kv_view(kv_all, data_rank, None), 4),
    ]
    greet("seq", "dp")
    context_gather.first()
    image_copies = [
        wires.send(image_ref.at[:, :, heads_of(peer)], image_all.at[k], "seq", peer)
        for k, peer in peers("seq")
        if k != late
    ]

    def late_image(kind):
        peer = lax.rem(rank + late, count)
        image_copies.append(
            wires.send(image_ref.at[kind, :, heads_of(peer)], image_all.at[late, kind], "seq", peer)
        )

    for copy in locals_:
        copy.start()

    token_copy.wait()
    for r in range(0, text, 32):
        block = tokens[r : r + 32, :].astype(f32)
        normed[r : r + 32, :] = rms_scale(block, gain_ref[...]).astype(bf16)

    def in_step(i, carry):
        slot = lax.rem(i, slots)
        in_copy(i, slot).wait()
        gate = jnp.dot(normed[...], in_tiles[slot, 0], preferred_element_type=f32)
        upward = jnp.dot(normed[...], in_tiles[slot, 1], preferred_element_type=f32)
        columns = pl.ds(pl.multiple_of(i * tile, 128), tile)
        hidden[:, columns] = (jax.nn.gelu(gate, approximate=True) * upward).astype(bf16)

        @pl.when(i + slots < tiles)
        def _():
            in_copy(i + slots, slot).start()

        return carry

    lax.fori_loop(0, tiles, in_step, 0)

    out_copy.wait()
    out_tile = tile_of(feat, 512)
    sums = []
    for k in [late] + [k for k in range(1, count) if k != late] + [0]:
        owner = lax.rem(rank + k, count)
        for t in range(0, feat, out_tile):
            columns = pl.ds(pl.multiple_of(owner * feat + t, 128), out_tile)
            part[k, :, t : t + out_tile] = jnp.dot(
                hidden[...], out_all[:, columns], preferred_element_type=f32
            ).astype(bf16)
            if k:
                sums.append(
                    wires.send(
                        part.at[k, :, t : t + out_tile], sum_slots.at[k - 1, :, t : t + out_tile], "seq", owner
                    )
                )

    context_gather.second()
    kv_gather.first()

    total = jnp.zeros((1, own_cols), f32)
    for r in range(0, depth, 128):
        block = proj_ref[r : r + 128, :].astype(f32) + lax.dot_general(
            down_ref[:, r : r + 128],
            up_ref[...],
            (((0,), (0,)), ((), ())),
            precision=lax.Precision.HIGHEST,
            preferred_element_type=f32,
        )
        direction[r : r + 128, :] = block
        total = total + jnp.sum(block * block, 0, keepdims=True)
    squares[...] = total
    square_copies = [wires.send(squares, square_slots.at[k - 1], "seq", peer) for k, peer in peers("seq")]

    context_gather.third()
    for copy in sums:
        copy.wait_recv()
    late_image(0)
    own = pl.ds(pl.multiple_of(rank * feat, 128), feat)
    for r in range(0, text, 32):
        total = part[0, r : r + 32, :].astype(f32)
        for k in range(1, count):
            total = total + sum_slots[k - 1, r : r + 32, :].astype(f32)
        encoded[r : r + 32, :] = (
            (tokens[r : r + 32, own].astype(f32) + total) * final_ref[:, own]
        ).astype(bf16)

    locals_[1].wait()
    context_gather.done()
    if flat:
        step = tile_of(width, 512)
        for c in range(0, width, step):
            context_part[:, c : c + step] = jnp.dot(
                encoded[...], context_all[:, c : c + step], preferred_element_type=f32
            ).astype(bf16)
    else:
        for d in range(devices):
            context_part[:, d * own_cols : (d + 1) * own_cols] = jnp.dot(
                encoded[...], context_all[d], preferred_element_type=f32
            ).astype(bf16)

    def block_of(index):
        return pl.ds(pl.multiple_of(index * rows, 16), rows)

    row_copies = [
        wires.send(context_part.at[block_of(peer)], row_slots.at[k - 1], "seq", peer) for k, peer in peers("seq")
    ]
    kv_gather.second()
    for copy in square_copies:
        copy.wait_recv()
    total = squares[...]
    for k in range(1, count):
        total = total + square_slots[k - 1]
    ratio = magnitude_ref[...] / jnp.sqrt(total + EPSILON)
    ratio_ref[...] = ratio
    for r in range(0, depth, 128):
        own_scaled[r : r + 128, :] = (direction[r : r + 128, :] * ratio).astype(bf16)
    own_scaled[depth:, :] = (up_ref[...] * ratio).astype(bf16)

    for copy in row_copies:
        copy.wait_recv()
    total = context_part[block_of(rank), :].astype(f32)
    for k in range(1, count):
        total = total + row_slots[k - 1].astype(f32)
    stage[...] = total.astype(bf16)

    chips = devices // 2
    chip = lax.div(data_rank, 2)
    sibling = place.at(other_core=True)
    prompt_copies = [
        wires.send(stage, prompts.at[j - 1], "dp", lax.rem(chip + j, chips) * 2 + place.core)
        for j in range(1, chips)
    ]
    shared = [wires.send(stage, sibling_prompts.at[0], "dp", sibling)]
    scaled_gather.first()
    local_scaled = local(own_scaled, scaled_view(gathered, data_rank, None), 5)
    local_scaled.start()
    late_image(1)
    for j in range(1, chips):
        prompt_copies[j - 1].wait_recv()
        shared.append(wires.send(prompts.at[j - 1], sibling_prompts.at[j], "dp", sibling))
    routed = jnp.where(owner_ref[data_rank] == data_rank, stage[...].astype(f32), 0.0)
    for j in range(1, chips):
        prompt = lax.rem(chip + chips - j, chips) * 2 + place.core
        routed = routed + jnp.where(owner_ref[prompt] == data_rank, prompts[j - 1].astype(f32), 0.0)
    for j in range(chips):
        shared[j].wait_recv()
        prompt = lax.rem(chip + chips - j, chips) * 2 + 1 - place.core
        routed = routed + jnp.where(owner_ref[prompt] == data_rank, sibling_prompts[j].astype(f32), 0.0)
    centre = jnp.mean(routed, -1, keepdims=True)
    spread = jnp.mean((routed - centre) * (routed - centre), -1, keepdims=True)
    layer_normed = (routed - centre) * lax.rsqrt(spread + EPSILON)
    final[...] = ((1.0 + scale_ref[...]) * layer_normed + shift_ref[...]).astype(bf16)
    text_copies = [wires.send(final, text_all.at[block_of(rank)], "seq", peer) for _, peer in peers("seq")]
    text_all[block_of(rank), :] = final[...]
    late_image(2)
    kv_gather.third()
    scaled_gather.second()
    locals_[2].wait()
    kv_gather.done()
    for copy in text_copies:
        copy.wait_recv()
    step = tile_of(kv_all.shape[1], 512)
    for c in range(0, kv_all.shape[1], step):
        key_value[:, c : c + step] = jnp.dot(
            text_all[...], kv_all[:, c : c + step], preferred_element_type=f32
        )
    scaled_gather.third()
    locals_[0].wait()
    local_scaled.wait()
    for copy in image_copies:
        copy.wait_recv()
    scaled_gather.done()
    wires.drain()


def wires_needed(count, pairs, sum_tiles):
    others = count - 1
    gathers = 3 * (pairs + 4 * (pairs - 1) + pairs + 2)
    return others + 3 + others * (sum_tiles + 3) + 4 * pairs + gathers


def front(owner, enc, gain, w_in, w_out, final_gain, context, kv, image, proj, down, up, magnitude, scale, shift):
    count, devices = lax.axis_size("seq"), lax.axis_size("dp")
    bf16, f32 = jnp.bfloat16, jnp.float32
    width_enc, hidden = w_in.shape[1:]
    feat = width_enc // count
    text = MAX_PROMPT
    width = scale.shape[1]
    rows = text // count
    kinds, image_rows, _ = image.shape
    head_width = width // count
    own_cols = proj.shape[1]
    scaled_rows = proj.shape[0] + up.shape[0]
    tile = tile_of(hidden, 256)
    slots = 3
    wires = wires_needed(count, devices // 4, feat // tile_of(feat, 512))
    any_ = pl.BlockSpec(memory_space=pl.ANY)
    gathered_shape = column_shape(devices, scaled_rows, own_cols)
    outs = pl.pallas_call(
        front_kernel,
        out_shape=[
            jax.ShapeDtypeStruct((count, kinds, image_rows, head_width), bf16),
            jax.ShapeDtypeStruct((text, kv.shape[1]), f32),
            jax.ShapeDtypeStruct(gathered_shape, bf16),
            jax.ShapeDtypeStruct((1, own_cols), f32),
        ],
        in_specs=[SMEM, any_, VMEM, any_, any_, VMEM, any_, any_, any_] + [VMEM] * 6,
        out_specs=[VMEM] * 4,
        scratch_shapes=[
            pltpu.VMEM((text, width_enc), bf16),
            pltpu.VMEM((text, width_enc), bf16),
            pltpu.VMEM((slots, 2, width_enc, tile), bf16),
            pltpu.VMEM((hidden, width_enc), bf16),
            pltpu.VMEM((text, hidden), bf16),
            pltpu.VMEM((count, text, feat), bf16),
            pltpu.VMEM((count - 1, text, feat), bf16),
            pltpu.VMEM((text, feat), bf16),
            pltpu.VMEM(column_shape(devices, context.shape[0], own_cols), bf16),
            pltpu.VMEM((kv.shape[0] * devices, kv.shape[1]), bf16),
            pltpu.VMEM((text, width), bf16),
            pltpu.VMEM((count - 1, rows, width), bf16),
            pltpu.VMEM((rows, width), bf16),
            pltpu.VMEM((devices // 2 - 1, rows, width), bf16),
            pltpu.VMEM((devices // 2, rows, width), bf16),
            pltpu.VMEM((rows, width), bf16),
            pltpu.VMEM((text, width), bf16),
            pltpu.VMEM(proj.shape, f32),
            pltpu.VMEM((1, own_cols), f32),
            pltpu.VMEM((count - 1, 1, own_cols), f32),
            pltpu.VMEM((scaled_rows, own_cols), bf16),
            pltpu.SemaphoreType.DMA((slots,)),
            pltpu.SemaphoreType.DMA((6,)),
            pltpu.SemaphoreType.DMA((wires,)),
            pltpu.SemaphoreType.DMA((wires,)),
        ],
        compiler_params=pltpu.CompilerParams(
            collective_id=1, has_side_effects=True, vmem_limit_bytes=62 * 2**20
        ),
    )(owner, enc, gain, w_in, w_out, final_gain, context, kv, image, proj, down, up, magnitude, scale, shift)
    image_all, key_value, gathered, ratio = outs
    if not flat_columns(own_cols):
        gathered = gathered.transpose(1, 0, 2).reshape(scaled_rows, -1)
    return image_all, key_value, gathered, ratio


def finish_kernel(
    att_ref, weight_ref, dora_ref, down_ref, grad_ref, grad_blocks_ref,
    image_out, size_out, cols_out, down_out,
    parts, stage_r, stage_l, got_r, got_l, up, up_slots, down_slots,
    cols, col_slots, col_stage, col_sums, rows_all, row_slots, row_stage, row_sums,
    size, size_slots, size_stage, size_sums,
    r_s, r_r, l_s, l_r, us, ur, ws, wr, cs, cr, c2s, c2r, as_, ar, a2s, a2r, gs, gr, g2s, g2r,
):
    count = lax.axis_size("seq")
    rank, data_rank = lax.axis_index("seq"), lax.axis_index("dp")
    rows, width = image_out.shape
    depth = att_ref.shape[1]
    half = width // 2
    f32, bf16 = jnp.float32, jnp.bfloat16
    over_rows = (((0,), (0,)), ((), ()))

    def product(k):
        block = att_ref[k * rows : (k + 1) * rows, :]
        for h in range(2):
            columns = slice(h * half, (h + 1) * half)
            parts[k, h] = jnp.dot(block, weight_ref[:depth, columns], preferred_element_type=f32).astype(bf16)

    def link(right, t, h):
        stage, got, ss, rs = (stage_r, got_r, r_s, r_r) if right else (stage_l, got_l, l_s, l_r)
        target = lax.rem(rank + (1 if right else count - 1), count)
        return pltpu.make_async_remote_copy(
            src_ref=stage.at[t - 1, h],
            dst_ref=got.at[t - 1, h],
            send_sem=ss.at[t - 1, h],
            recv_sem=rs.at[t - 1, h],
            device_id={"seq": target},
            device_id_type=pl.DeviceIdType.MESH,
        )

    def chain(t, h):
        for right in (True, False):
            stage, got = (stage_r, got_r) if right else (stage_l, got_l)
            place = rank if right else count - 1 - rank
            part = t if right else count - t

            if t == 1:

                @pl.when(place == 0)
                def _():
                    stage[0, h] = parts[part, h]
                    link(right, 1, h).start()

            else:

                @pl.when(place == 0)
                def _():
                    stage[t - 1, h] = parts[part, h]
                    link(right, t, h).start()

                @pl.when((place >= 1) & (place <= t - 1))
                def _():
                    link(right, t - 1, h).wait_recv()
                    stage[t - 1, h] = (
                        parts[part, h].astype(f32) + got[t - 2, h].astype(f32)
                    ).astype(bf16)
                    link(right, t, h).start()

    greet("seq", "dp")
    done = {0}
    for k in (1, count - 1):
        if k not in done:
            product(k)
            done.add(k)
    for h in range(2):
        chain(1, h)

    ups = jnp.dot(att_ref[...], dora_ref[...], preferred_element_type=f32).astype(bf16)
    for k in range(count):
        up[k] = ups[k * rows : (k + 1) * rows]
    small = []
    for k in range(1, count):
        before = lax.rem(rank + count - k, count)
        small.append(send(up.at[k], up_slots.at[k - 1], us.at[k - 1], ur.at[k - 1], "seq", before))
        after = lax.rem(rank + k, count)
        small.append(send(down_ref, down_slots.at[k - 1], ws.at[k - 1], wr.at[k - 1], "seq", after))
    for t in range(2, count):
        for k in (t, count - t):
            if k not in done:
                product(k)
                done.add(k)
    product(0)
    finish(small)
    up_total = up[0].astype(f32)
    for k in range(1, count):
        up_total = up_total + up_slots[k - 1].astype(f32)
    up_total = up_total.astype(bf16)
    blocks, block_rows = rows_all.shape[0], rows_all.shape[1]
    for j in range(blocks):
        cols[j] = lax.dot_general(
            up_total, grad_blocks_ref[j], over_rows, preferred_element_type=f32
        ).astype(bf16)
    grad_rows = lax.dot_general(att_ref[:rows, :], down_ref[...], over_rows, preferred_element_type=f32)
    for k in range(1, count):
        grad_rows = grad_rows + lax.dot_general(
            att_ref[k * rows : (k + 1) * rows, :], down_slots[k - 1], over_rows, preferred_element_type=f32
        )
    for j in range(blocks):
        rows_all[j] = grad_rows[j * block_rows : (j + 1) * block_rows].astype(bf16)
    first = []
    for k, peer in peers("dp"):
        first.append(send(cols.at[peer], col_slots.at[k - 1], cs.at[k - 1], cr.at[k - 1], "dp", peer))
        first.append(send(rows_all.at[peer], row_slots.at[k - 1], as_.at[k - 1], ar.at[k - 1], "dp", peer))
    second = []
    for t in range(2, count):
        for h in range(2):
            chain(t, h)
        if t == 2:
            finish(first)
            col_total = cols[data_rank].astype(f32)
            row_total = rows_all[data_rank].astype(f32)
            for k, _ in peers("dp"):
                col_total = col_total + col_slots[k - 1].astype(f32)
                row_total = row_total + row_slots[k - 1].astype(f32)
            col_stage[...] = col_total.astype(bf16)
            row_stage[...] = row_total.astype(bf16)
            for k, peer in peers("seq"):
                second.append(send(col_stage, col_sums.at[k - 1], c2s.at[k - 1], c2r.at[k - 1], "seq", peer))
            for k, peer in peers("dp"):
                second.append(
                    send(row_stage, row_sums.at[data_rank], a2s.at[k - 1], a2r.at[k - 1], "dp", peer)
                )
            row_sums[data_rank] = row_stage[...]

    for h in range(2):

        @pl.when(rank >= 1)
        def _():
            link(True, count - 1, h).wait_recv()

        @pl.when(rank <= count - 2)
        def _():
            link(False, count - 1, h).wait_recv()

        columns = slice(h * half, (h + 1) * half)
        total = parts[0, h].astype(f32)
        total = total + jnp.where(rank >= 1, got_r[count - 2, h].astype(f32), 0.0)
        total = total + jnp.where(rank <= count - 2, got_l[count - 2, h].astype(f32), 0.0)
        image_out[:, columns] = total.astype(bf16)
        size[:, columns] = jnp.sum(grad_ref[:, columns].astype(f32) * total, 0, keepdims=True)
    last = [
        send(size, size_slots.at[k - 1], gs.at[k - 1], gr.at[k - 1], "dp", peer) for k, peer in peers("dp")
    ]
    finish(second)
    col_total = col_stage[...].astype(f32)
    for k, _ in peers("seq"):
        col_total = col_total + col_sums[k - 1].astype(f32)
    cols_out[...] = col_total
    down_out[...] = row_sums[...].astype(f32)
    finish(last)
    size_total = size[...]
    for k, _ in peers("dp"):
        size_total = size_total + size_slots[k - 1]
    size_stage[...] = size_total
    finish(
        [
            send(size_stage, size_sums.at[k - 1], g2s.at[k - 1], g2r.at[k - 1], "seq", peer)
            for k, peer in peers("seq")
        ]
    )
    for k, _ in peers("seq"):
        size_total = size_total + size_sums[k - 1]
    size_out[...] = size_total
    for t in range(1, count):
        for h in range(2):

            @pl.when(rank <= t - 1)
            def _():
                link(True, t, h).wait_send()

            @pl.when(count - 1 - rank <= t - 1)
            def _():
                link(False, t, h).wait_send()


def finish_step(attended, gathered, dora, down, grad, grad_blocks):
    count, data_devices = lax.axis_size("seq"), lax.axis_size("dp")
    depth, (rows, width) = attended.shape[1], grad.shape
    rank, own_cols = down.shape[1], grad_blocks.shape[2]
    block_rows = depth // data_devices
    f32, bf16 = jnp.float32, jnp.bfloat16
    halves = (rows, width // 2)
    return pl.pallas_call(
        finish_kernel,
        out_shape=[
            jax.ShapeDtypeStruct((rows, width), bf16),
            jax.ShapeDtypeStruct((1, width), f32),
            jax.ShapeDtypeStruct((rank, own_cols), f32),
            jax.ShapeDtypeStruct((data_devices, block_rows, rank), f32),
        ],
        in_specs=[VMEM] * 6,
        out_specs=[VMEM] * 4,
        scratch_shapes=[
            pltpu.VMEM((count, 2) + halves, bf16),
        ]
        + [pltpu.VMEM((count - 1, 2) + halves, bf16)] * 4
        + [
            pltpu.VMEM((count, rows, rank), bf16),
            pltpu.VMEM((count - 1, rows, rank), bf16),
            pltpu.VMEM((count - 1, rows, rank), bf16),
            pltpu.VMEM((data_devices, rank, own_cols), bf16),
            pltpu.VMEM((data_devices - 1, rank, own_cols), bf16),
            pltpu.VMEM((rank, own_cols), bf16),
            pltpu.VMEM((count - 1, rank, own_cols), bf16),
            pltpu.VMEM((data_devices, block_rows, rank), bf16),
            pltpu.VMEM((data_devices - 1, block_rows, rank), bf16),
            pltpu.VMEM((block_rows, rank), bf16),
            pltpu.VMEM((data_devices, block_rows, rank), bf16),
            pltpu.VMEM((1, width), f32),
            pltpu.VMEM((data_devices - 1, 1, width), f32),
            pltpu.VMEM((1, width), f32),
            pltpu.VMEM((count - 1, 1, width), f32),
        ]
        + [pltpu.SemaphoreType.DMA((count - 1, 2))] * 4
        + sems(count - 1) * 2
        + sems(data_devices - 1)
        + sems(count - 1)
        + sems(data_devices - 1) * 2
        + sems(data_devices - 1)
        + sems(count - 1),
        compiler_params=pltpu.CompilerParams(
            collective_id=3, has_side_effects=True, vmem_limit_bytes=58 * 2**20
        ),
    )(attended, gathered, dora, down, grad, grad_blocks)


def on_device(
    enc_states,
    lengths,
    prompt_owner_sample,
    t5_gain,
    t5_in_weight,
    t5_out_weight,
    t5_final_gain,
    context_weight,
    text_shift,
    text_scale,
    kv_weight,
    text_key_gain,
    image_query_key_value,
    image_qk_gain,
    proj_weight,
    dora_a,
    dora_b,
    magnitude,
    grad_out,
):
    data_rank = lax.axis_index("dp")
    bf16, f32 = jnp.bfloat16, jnp.float32
    image_all, key_value, gathered, ratio = front(
        prompt_owner_sample,
        enc_states,
        t5_gain[None],
        t5_in_weight,
        t5_out_weight,
        t5_final_gain[None],
        context_weight,
        kv_weight.reshape(kv_weight.shape[0], -1),
        jnp.transpose(image_query_key_value[0], (1, 0, 2)),
        proj_weight,
        dora_a.T,
        dora_b,
        magnitude[None],
        text_scale,
        text_shift,
    )
    ratio = ratio[0]
    scaled_up = gathered[dora_a.shape[0] :]
    diffusion_length = jnp.sum(jnp.where(prompt_owner_sample == data_rank, lengths, 0))
    attended = attention(diffusion_length, text_key_gain, image_qk_gain, key_value, image_all)

    down = lax.dot_general(
        grad_out[0], scaled_up, (((1,), (1,)), ((), ())), preferred_element_type=f32
    ).astype(bf16)
    data_devices = lax.axis_size("dp")
    grad_blocks = grad_out[0].reshape(grad_out.shape[1], data_devices, -1).transpose(1, 0, 2)
    image_out, sizes, column_sums, grad_a = finish_step(
        attended, gathered, dora_a.astype(bf16), down, grad_out[0], grad_blocks
    )
    grad_a = grad_a.reshape(-1, dora_b.shape[0])
    grad_b = column_sums * ratio
    own_cols = magnitude.shape[0]
    grad_magnitude = lax.dynamic_slice_in_dim(sizes[0], data_rank * own_cols, own_cols, 0) / magnitude
    return (image_out[None], grad_a, grad_b, grad_magnitude)


def solution(mesh):
    mapped = jax.shard_map(
        on_device,
        mesh=mesh,
        in_specs=(
            P("dp", None, None),
            P(),
            P(),
            P(),
            P(None, None, "seq"),
            P("seq", None),
            P(),
            P("seq", "dp"),
            P("dp", None),
            P("dp", None),
            P("dp", None, "seq"),
            P(),
            P("dp", "seq", None, None),
            P(),
            P("seq", "dp"),
            P("seq", None),
            P(None, "dp"),
            P("dp"),
            P("dp", "seq", None),
        ),
        out_specs=(P("dp", "seq", None), P("seq", None), P(None, "dp"), P("dp")),
        check_vma=False,
    )
    return mapped
```

profile of v0, /device:TPU:0, one launch (start us, length us, event | category | flops | bytes accessed | tf_op | source)
XLA Modules:
  0.0 229.2 jit_solution(518155271359911642)
XLA Ops:
  0.6 2.5 %copy.36 = bf16[48,8,2,768]{3,1,2,0:T(8,128)(2,1)} copy(bf16[48,8,2,768]{3,2,1,0:T(2,128)(2,1)} %bitcast.23) | data formatting | bytes 2359296
  3.1 1.2 broadcast_in_dim.19.magnitude_ref
  4.4 124.5 %shard_map.210 = (bf16[4,3,128,768]{3,2,1,0:T(8,128)(2,1)}, f32[128,1536]{1,0:T(8,128)}, bf16[832,3072]{1,0:T(8,128)(2,1)}, f32[1,384]{1,0:T(1,128)}) custom-call(s32[8]{0:T(128)} %owner_ref.1, bf16[1,256,4096]{2,1,0:T(8,128)(2,1)} %enc_ref.1, f32[1,4096]{1,0:T(1,128)} %bitcast.28, bf16[2,4096,1280]{2,1,0:T(8,128)(2,1)} %in_ref.1, ...), custom_call_target="tpu_custom_call" | custom-call | tf_op jit(solution)/shard_map/pallas_call | solution.py:493
  128.9 0.0 copy-start.1
  128.9 0.0 copy-done.3
  129.0 0.0 copy-done.5
  129.0 0.6 fusion.1
  129.6 7.7 %shard_map.211.att_ref = bf16[512,768]{1,0:T(8,128)(2,1)} custom-call(s32[1]{0:T(128)} %bitcast.length_ref, f32[1,128]{1,0:T(1,128)} %bitcast.30, f32[2,128]{1,0:T(2,128)} %image_gain_ref.1, f32[128,1536]{1,0:T(8,128)} %get-tuple-element.12.text_key_ref.text_value_ref, f32[128,1536]{1,0:T(8,128)} %get-tuple-element.12.text_key_ref.text_value_ref, ...), custom_call_target="tpu_custom_call" | custom-call | flops 1006632960 | bytes 3145728 | tf_op jit(solution)/shard_map/pallas_call | solution.py:51
  137.3 0.0 copy-done
  137.3 1.4 convolution_convert_fusion
  138.7 0.7 copy.31
  139.4 0.4 copy.32
  139.8 0.0 copy-start.2
  139.8 0.0 copy-start.4
  139.8 1.2 copy.33
  141.0 0.0 copy-done.1
  141.0 0.8 copy.34.dora_ref
  141.8 80.6 %shard_map.212 = (bf16[128,3072]{1,0:T(8,128)(2,1)}, f32[1,3072]{1,0:T(1,128)}, f32[64,384]{1,0:T(8,128)}, f32[8,96,64]{2,1,0:T(8,128)}) custom-call(bf16[512,768]{1,0:T(8,128)(2,1)} %shard_map.211.att_ref, bf16[832,3072]{1,0:T(8,128)(2,1)} %get-tuple-element.14.weight_ref, bf16[768,64]{1,0:T(8,128)(2,1)} %copy.34.dora_ref, bf16[128,64]{1,0:T(8,128)(2,1)} %bitcast.27, ...), custom_call_target="tpu_custom_call" | custom-call | tf_op jit(solution)/shard_map/pallas_call | solution.py:726
  222.5 0.7 dynamic-slice_reduce_fusion
  223.2 0.6 div.3
  223.7 0.0 copy-done.4
  223.8 1.5 broadcast_multiply_fusion
  225.3 1.8 copy.35
  227.1 2.1 copy.38
  (6 shorter events, 0.0 us)
Async XLA Ops:
  4.4 124.6 %copy-start.3 = (s32[8]{0:T(128)S(1)}, s32[8]{0:T(128)}, u32[]{:S(2)}) copy-start(s32[8]{0:T(128)} %owner_ref.1) | copy-start | bytes 100
  4.4 124.6 %copy-start.5 = (s32[8]{0:T(128)S(1)}, s32[8]{0:T(128)}, u32[]{:S(2)}) copy-start(s32[8]{0:T(128)} %param.20) | copy-start | bytes 100
  4.4 133.0 %copy-start = (bf16[1,128,3072]{2,1,0:T(8,128)(2,1)S(1)}, bf16[1,128,3072]{2,1,0:T(8,128)(2,1)}, u32[]{:S(2)}) copy-start(bf16[1,128,3072]{2,1,0:T(8,128)(2,1)} %param.37) | copy-start | bytes 2359300
  128.9 12.1 %copy-start.1 = (f32[768,64]{0,1:T(8,128)S(1)}, f32[768,64]{0,1:T(8,128)}, u32[]{:S(2)}) copy-start(f32[768,64]{0,1:T(8,128)} %param.34) | copy-start | bytes 589828
  139.8 83.3 %copy-start.2 = (f32[384]{0:T(512)S(1)}, f32[384]{0:T(512)}, u32[]{:S(2)}) copy-start(f32[384]{0:T(512)} %param.36) | copy-start | bytes 4612
  139.8 83.9 %copy-start.4 = (f32[1,384]{1,0:T(1,128)S(1)}, f32[1,384]{1,0:T(1,128)}, u32[]{:S(2)}) copy-start(f32[1,384]{1,0:T(1,128)} %get-tuple-element.18) | copy-start | bytes 4612
where the time goes:
time: 230 us; the launch traced here: 229 us
  Pallas kernels  213 us (93%)
  local copies, waits for them, and re-layouts  11.4 us (5%)
  other arithmetic  2.79 us (1%)
    pallas_call x1, Pallas kernels, front(): pl.pallas_call(front_kernel, out_shape=[jax.ShapeDtypeStruct((count, kind...  125 us
    pallas_call x1, Pallas kernels, finish_step(): pl.pallas_call(finish_kernel, out_shape=[jax.ShapeDtypeStruct((rows, widt...  80.6 us
    pallas_call x1, Pallas kernels, attention(): pl.pallas_call(attention_kernel, grid=(heads,), out_shape=jax.ShapeDtypeS...  7.72 us
    unnamed x16, local copies, waits for them, and re-layouts  6.77 us

commit v1 on v0

--- a/solution.py
+++ b/solution.py
@@ -14,59 +14,6 @@
 
 def rms_scale(values, gain):
     return values * lax.rsqrt(jnp.mean(values * values, -1, keepdims=True) + EPSILON) * gain
-
-
-def attention_kernel(length_ref, text_gain_ref, image_gain_ref, text_key_ref, text_value_ref, image_ref, out_ref):
-    def stacked(kind):
-        return jnp.concatenate([image_ref[k, kind] for k in range(image_ref.shape[0])], 0)
-
-    queries = rms_scale(stacked(0).astype(jnp.float32), image_gain_ref[0:1, :])
-    queries = (queries).astype(jnp.bfloat16)
-    key_image = rms_scale(stacked(1).astype(jnp.float32), image_gain_ref[1:2, :]).astype(jnp.bfloat16)
-    key_text = rms_scale(text_key_ref[...], text_gain_ref[...]).astype(jnp.bfloat16)
-    scale = 1.0 / math.sqrt(HD)
-    dims = (((1,), (1,)), ((), ()))
-    text_scores = lax.dot_general(queries, key_text, dims, preferred_element_type=jnp.float32) * scale
-    image_scores = lax.dot_general(queries, key_image, dims, preferred_element_type=jnp.float32) * scale
-    position = lax.broadcasted_iota(jnp.int32, text_scores.shape, 1)
-    text_weight = jnp.where(position < length_ref[0], jnp.exp(text_scores), 0.0)
-    image_weight = jnp.exp(image_scores)
-    denominator = jnp.sum(text_weight, -1, keepdims=True) + jnp.sum(image_weight, -1, keepdims=True)
-    mixture = jnp.dot(
-        text_weight.astype(jnp.bfloat16),
-        text_value_ref[...].astype(jnp.bfloat16),
-        preferred_element_type=jnp.float32,
-    )
-    mixture = mixture + jnp.dot(
-        image_weight.astype(jnp.bfloat16), stacked(2), preferred_element_type=jnp.float32
-    )
-    out_ref[...] = (mixture / denominator).astype(jnp.bfloat16)
-
-
-def attention(length, text_gain, image_gain, key_value, image_all):
-    blocks, kinds, rows, width = image_all.shape
-    heads = width // HD
-    text = key_value.shape[0]
-    vmem = lambda shape, index: pl.BlockSpec(shape, index)
-    return pl.pallas_call(
-        attention_kernel,
-        grid=(heads,),
-        out_shape=jax.ShapeDtypeStruct((blocks * rows, width), jnp.bfloat16),
-        in_specs=[
-            pl.BlockSpec(memory_space=pltpu.SMEM),
-            vmem((1, HD), lambda h: (0, 0)),
-            vmem((2, HD), lambda h: (0, 0)),
-            vmem((text, HD), lambda h: (0, h)),
-            vmem((text, HD), lambda h: (0, heads + h)),
-            vmem((blocks, kinds, rows, HD), lambda h: (0, 0, 0, h)),
-        ],
-        out_specs=vmem((blocks * rows, HD), lambda h: (0, h)),
-        cost_estimate=pl.CostEstimate(
-            flops=4 * heads * blocks * rows * (blocks * rows + text) * HD,
-            bytes_accessed=8 * blocks * rows * width,
-            transcendentals=heads * blocks * rows * (blocks * rows + text),
-        ),
-    )(length.reshape(1), text_gain.reshape(1, HD), image_gain, key_value, key_value, image_all)
 
 
 def peers(axis):
@@ -86,36 +33,8 @@
     pl.semaphore_wait(barrier, count)
 
 
-def send(source, target, send_sem, recv_sem, axis, peer):
-    copy = pltpu.make_async_remote_copy(
-        src_ref=source,
-        dst_ref=target,
-        send_sem=send_sem,
-        recv_sem=recv_sem,
-        device_id={axis: peer},
-        device_id_type=pl.DeviceIdType.MESH,
-    )
-    copy.start()
-    return copy
-
-
-def finish(copies):
-    for copy in copies:
-        copy.wait()
-
-
-def sems(count):
-    return [pltpu.SemaphoreType.DMA((count,)), pltpu.SemaphoreType.DMA((count,))]
-
-
 VMEM = pl.BlockSpec(memory_space=pltpu.VMEM)
 SMEM = pl.BlockSpec(memory_space=pltpu.SMEM)
-
-
-def params(collective_id):
-    return pltpu.CompilerParams(
-        collective_id=collective_id, has_side_effects=True, vmem_limit_bytes=40 * 2**20
-    )
 
 
 MESH = pl.DeviceIdType.MESH
@@ -537,234 +456,278 @@
     return image_all, key_value, gathered, ratio
 
 
-def finish_kernel(
-    att_ref, weight_ref, dora_ref, down_ref, grad_ref, grad_blocks_ref,
-    image_out, size_out, cols_out, down_out,
-    parts, stage_r, stage_l, got_r, got_l, up, up_slots, down_slots,
+def back_kernel(
+    owner_ref, lengths_ref, text_gain_ref, image_gain_ref, key_value_ref, image_ref, weight_ref, dora_ref,
+    grad_ref, ratio_ref, magnitude_ref,
+    image_out, down_out, cols_out, size_out,
+    keys, values, attended, parts, slots, down, up, up_slots, down_slots,
     cols, col_slots, col_stage, col_sums, rows_all, row_slots, row_stage, row_sums,
     size, size_slots, size_stage, size_sums,
-    r_s, r_r, l_s, l_r, us, ur, ws, wr, cs, cr, c2s, c2r, as_, ar, a2s, a2r, gs, gr, g2s, g2r,
+    chain_send, chain_recv, send_sems, recv_sems,
 ):
-    count = lax.axis_size("seq")
+    count, devices = lax.axis_size("seq"), lax.axis_size("dp")
     rank, data_rank = lax.axis_index("seq"), lax.axis_index("dp")
     rows, width = image_out.shape
-    depth = att_ref.shape[1]
+    depth = image_ref.shape[3]
+    text = key_value_ref.shape[0]
+    heads = depth // HD
     half = width // 2
+    own_cols = ratio_ref.shape[1]
+    block_rows = depth // devices
     f32, bf16 = jnp.float32, jnp.bfloat16
     over_rows = (((0,), (0,)), ((), ()))
-
-    def product(k):
-        block = att_ref[k * rows : (k + 1) * rows, :]
+    over_columns = (((1,), (1,)), ((), ()))
+    wires = Wires(send_sems, recv_sems)
+    near = 1 - lax.div(rank, count // 2)
+
+    def target_of(step, right):
+        return right * (count - 1 - step) + (1 - right) * step
+
+    def block_of(owner):
+        return lax.rem(rank + count - owner, count)
+
+    def link(owner, h, right):
+        index = (right * count + owner) * 2 + h
+        return pltpu.make_async_remote_copy(
+            src_ref=parts.at[owner, h],
+            dst_ref=slots.at[right, owner, h],
+            send_sem=chain_send.at[owner * 2 + h],
+            recv_sem=chain_recv.at[index],
+            device_id={"seq": jnp.clip(rank + 2 * right - 1, 0, count - 1)},
+            device_id_type=MESH,
+        )
+
+    def begin(step):
+        owner = target_of(step, near)
+
+        @pl.when((rank == 0) | (rank == count - 1))
+        def _():
+            for h in range(2):
+                link(owner, h, near).start()
+
+    def forward(step, right):
+        owner = target_of(step, right)
+        ahead = right * (owner - rank) + (1 - right) * (rank - owner)
+        behind = right * rank + (1 - right) * (count - 1 - rank)
+
+        @pl.when((ahead > 0) & (behind > 0))
+        def _():
+            for h in range(2):
+                link(owner, h, right).wait_recv()
+                parts[owner, h] = (parts[owner, h].astype(f32) + slots[right, owner, h].astype(f32)).astype(bf16)
+                link(owner, h, right).start()
+
+    greet("seq", "dp")
+    down[...] = lax.dot_general(
+        grad_ref[...], weight_ref[depth:, :], over_columns, preferred_element_type=f32
+    ).astype(bf16)
+    small = []
+    for k, peer in peers("seq"):
+        small.append(wires.send(down, down_slots.at[k - 1], "seq", peer))
+
+    length = jnp.int32(0)
+    for p in range(devices):
+        length = length + jnp.where(owner_ref[p] == data_rank, lengths_ref[p], 0)
+
+    def head(h):
+        return pl.ds(pl.multiple_of(h * HD, HD), HD)
+
+    def key_step(h, carry):
+        keys[:text, head(h)] = rms_scale(key_value_ref[:, head(h)], text_gain_ref[...]).astype(bf16)
+        for k in range(count):
+            start = text + k * rows
+            keys[start : start + rows, head(h)] = rms_scale(
+                image_ref[k, 1, :, head(h)].astype(f32), image_gain_ref[1:2, :]
+            ).astype(bf16)
+        return carry
+
+    lax.fori_loop(0, heads, key_step, 0)
+    values[:text, :] = key_value_ref[:, depth:].astype(bf16)
+    for k in range(count):
+        start = text + k * rows
+        values[start : start + rows, :] = image_ref[k, 2]
+    scale = 1.0 / math.sqrt(HD)
+
+    for step in range(count):
+        owner = target_of(step, near)
+        block = block_of(owner)
+        block_slice = pl.ds(pl.multiple_of(block * rows, 16), rows)
+
+        def head_step(h, carry):
+            queries = rms_scale(
+                image_ref[block, 0, :, head(h)].astype(f32), image_gain_ref[0:1, :]
+            ).astype(bf16)
+            scores = lax.dot_general(queries, keys[:, head(h)], over_columns, preferred_element_type=f32) * scale
+            position = lax.broadcasted_iota(jnp.int32, scores.shape, 1)
+            weight = jnp.where((position < length) | (position >= text), jnp.exp(scores), 0.0)
+            denominator = jnp.sum(weight, -1, keepdims=True)
+            mixture = jnp.dot(weight.astype(bf16), values[:, head(h)], preferred_element_type=f32)
+            attended[block_slice, head(h)] = (mixture / denominator).astype(bf16)
+            return carry
+
+        lax.fori_loop(0, heads, head_step, 0)
         for h in range(2):
             columns = slice(h * half, (h + 1) * half)
-            parts[k, h] = jnp.dot(block, weight_ref[:depth, columns], preferred_element_type=f32).astype(bf16)
-
-    def link(right, t, h):
-        stage, got, ss, rs = (stage_r, got_r, r_s, r_r) if right else (stage_l, got_l, l_s, l_r)
-        target = lax.rem(rank + (1 if right else count - 1), count)
-        return pltpu.make_async_remote_copy(
-            src_ref=stage.at[t - 1, h],
-            dst_ref=got.at[t - 1, h],
-            send_sem=ss.at[t - 1, h],
-            recv_sem=rs.at[t - 1, h],
-            device_id={"seq": target},
-            device_id_type=pl.DeviceIdType.MESH,
-        )
-
-    def chain(t, h):
-        for right in (True, False):
-            stage, got = (stage_r, got_r) if right else (stage_l, got_l)
-            place = rank if right else count - 1 - rank
-            part = t if right else count - t
-
-            if t == 1:
-
-                @pl.when(place == 0)
-                def _():
-                    stage[0, h] = parts[part, h]
-                    link(right, 1, h).start()
-
-            else:
-
-                @pl.when(place == 0)
-                def _():
-                    stage[t - 1, h] = parts[part, h]
-                    link(right, t, h).start()
-
-                @pl.when((place >= 1) & (place <= t - 1))
-                def _():
-                    link(right, t - 1, h).wait_recv()
-                    stage[t - 1, h] = (
-                        parts[part, h].astype(f32) + got[t - 2, h].astype(f32)
-                    ).astype(bf16)
-                    link(right, t, h).start()
-
-    greet("seq", "dp")
-    done = {0}
-    for k in (1, count - 1):
-        if k not in done:
-            product(k)
-            done.add(k)
-    for h in range(2):
-        chain(1, h)
-
-    ups = jnp.dot(att_ref[...], dora_ref[...], preferred_element_type=f32).astype(bf16)
+            parts[owner, h] = jnp.dot(
+                attended[block_slice, :], weight_ref[:depth, columns], preferred_element_type=f32
+            ).astype(bf16)
+        if step == 0:
+            begin(0)
+
+    dora = dora_ref[...].astype(bf16)
+    ups = lax.dot_general(attended[...], dora, over_columns, preferred_element_type=f32).astype(bf16)
     for k in range(count):
         up[k] = ups[k * rows : (k + 1) * rows]
-    small = []
     for k in range(1, count):
         before = lax.rem(rank + count - k, count)
-        small.append(send(up.at[k], up_slots.at[k - 1], us.at[k - 1], ur.at[k - 1], "seq", before))
-        after = lax.rem(rank + k, count)
-        small.append(send(down_ref, down_slots.at[k - 1], ws.at[k - 1], wr.at[k - 1], "seq", after))
-    for t in range(2, count):
-        for k in (t, count - t):
-            if k not in done:
-                product(k)
-                done.add(k)
-    product(0)
-    finish(small)
+        small.append(wires.send(up.at[k], up_slots.at[k - 1], "seq", before))
+    for step in range(1, count - 2):
+        begin(step)
+    forward(0, near)
+    for copy in small:
+        copy.wait_recv()
     up_total = up[0].astype(f32)
     for k in range(1, count):
         up_total = up_total + up_slots[k - 1].astype(f32)
     up_total = up_total.astype(bf16)
-    blocks, block_rows = rows_all.shape[0], rows_all.shape[1]
-    for j in range(blocks):
-        cols[j] = lax.dot_general(
-            up_total, grad_blocks_ref[j], over_rows, preferred_element_type=f32
-        ).astype(bf16)
-    grad_rows = lax.dot_general(att_ref[:rows, :], down_ref[...], over_rows, preferred_element_type=f32)
+    column_grad = lax.dot_general(up_total, grad_ref[...], over_rows, preferred_element_type=f32).astype(bf16)
+    for j in range(devices):
+        cols[j] = column_grad[:, j * own_cols : (j + 1) * own_cols]
+    row_grad = lax.dot_general(down[...], attended[:rows, :], over_rows, preferred_element_type=f32)
     for k in range(1, count):
-        grad_rows = grad_rows + lax.dot_general(
-            att_ref[k * rows : (k + 1) * rows, :], down_slots[k - 1], over_rows, preferred_element_type=f32
+        row_grad = row_grad + lax.dot_general(
+            down_slots[k - 1], attended[k * rows : (k + 1) * rows, :], over_rows, preferred_element_type=f32
         )
-    for j in range(blocks):
-        rows_all[j] = grad_rows[j * block_rows : (j + 1) * block_rows].astype(bf16)
+    for j in range(devices):
+        rows_all[j] = row_grad[:, j * block_rows : (j + 1) * block_rows].astype(bf16)
     first = []
     for k, peer in peers("dp"):
-        first.append(send(cols.at[peer], col_slots.at[k - 1], cs.at[k - 1], cr.at[k - 1], "dp", peer))
-        first.append(send(rows_all.at[peer], row_slots.at[k - 1], as_.at[k - 1], ar.at[k - 1], "dp", peer))
+        first.append(wires.send(cols.at[peer], col_slots.at[k - 1], "dp", peer))
+        first.append(wires.send(rows_all.at[peer], row_slots.at[k - 1], "dp", peer))
+    for copy in first:
+        copy.wait_recv()
+    col_total = cols[data_rank].astype(f32)
+    row_total = rows_all[data_rank].astype(f32)
+    for k, _ in peers("dp"):
+        col_total = col_total + col_slots[k - 1].astype(f32)
+        row_total = row_total + row_slots[k - 1].astype(f32)
+    col_stage[...] = col_total.astype(bf16)
+    row_stage[...] = row_total.astype(bf16)
     second = []
-    for t in range(2, count):
-        for h in range(2):
-            chain(t, h)
-        if t == 2:
-            finish(first)
-            col_total = cols[data_rank].astype(f32)
-            row_total = rows_all[data_rank].astype(f32)
-            for k, _ in peers("dp"):
-                col_total = col_total + col_slots[k - 1].astype(f32)
-                row_total = row_total + row_slots[k - 1].astype(f32)
-            col_stage[...] = col_total.astype(bf16)
-            row_stage[...] = row_total.astype(bf16)
-            for k, peer in peers("seq"):
-                second.append(send(col_stage, col_sums.at[k - 1], c2s.at[k - 1], c2r.at[k - 1], "seq", peer))
-            for k, peer in peers("dp"):
-                second.append(
-                    send(row_stage, row_sums.at[data_rank], a2s.at[k - 1], a2r.at[k - 1], "dp", peer)
-                )
-            row_sums[data_rank] = row_stage[...]
-
+    for k, peer in peers("seq"):
+        second.append(wires.send(col_stage, col_sums.at[k - 1], "seq", peer))
+    for k, peer in peers("dp"):
+        second.append(wires.send(row_stage, row_sums.at[data_rank], "dp", peer))
+    row_sums[data_rank] = row_stage[...]
+    begin(count - 2)
+    forward(0, 1 - near)
+    for step in range(1, count - 1):
+        forward(step, near)
+        forward(step, 1 - near)
+
+    sums = []
     for h in range(2):
 
         @pl.when(rank >= 1)
         def _():
-            link(True, count - 1, h).wait_recv()
+            link(rank, h, 1).wait_recv()
 
         @pl.when(rank <= count - 2)
         def _():
-            link(False, count - 1, h).wait_recv()
+            link(rank, h, 0).wait_recv()
 
         columns = slice(h * half, (h + 1) * half)
-        total = parts[0, h].astype(f32)
-        total = total + jnp.where(rank >= 1, got_r[count - 2, h].astype(f32), 0.0)
-        total = total + jnp.where(rank <= count - 2, got_l[count - 2, h].astype(f32), 0.0)
+        total = parts[rank, h].astype(f32)
+        total = total + jnp.where(rank >= 1, slots[1, rank, h].astype(f32), 0.0)
+        total = total + jnp.where(rank <= count - 2, slots[0, rank, h].astype(f32), 0.0)
         image_out[:, columns] = total.astype(bf16)
-        size[:, columns] = jnp.sum(grad_ref[:, columns].astype(f32) * total, 0, keepdims=True)
-    last = [
-        send(size, size_slots.at[k - 1], gs.at[k - 1], gr.at[k - 1], "dp", peer) for k, peer in peers("dp")
-    ]
-    finish(second)
+        sums.append(jnp.sum(grad_ref[:, columns].astype(f32) * total, 0, keepdims=True))
+    per_half = devices // 2
+    for d in range(devices):
+        start = (d % per_half) * own_cols
+        size[d] = sums[d // per_half][:, start : start + own_cols]
+    last = [wires.send(size.at[peer], size_slots.at[k - 1], "dp", peer) for k, peer in peers("dp")]
+    for copy in second:
+        copy.wait_recv()
     col_total = col_stage[...].astype(f32)
     for k, _ in peers("seq"):
         col_total = col_total + col_sums[k - 1].astype(f32)
-    cols_out[...] = col_total
-    down_out[...] = row_sums[...].astype(f32)
-    finish(last)
-    size_total = size[...]
+    cols_out[...] = col_total * ratio_ref[...]
+    for d in range(devices):
+        down_out[:, d * block_rows : (d + 1) * block_rows] = row_sums[d].astype(f32)
+    for copy in last:
+        copy.wait_recv()
+    size_total = size[data_rank]
     for k, _ in peers("dp"):
         size_total = size_total + size_slots[k - 1]
     size_stage[...] = size_total
-    finish(
-        [
-            send(size_stage, size_sums.at[k - 1], g2s.at[k - 1], g2r.at[k - 1], "seq", peer)
-            for k, peer in peers("seq")
-        ]
-    )
+    last = [wires.send(size_stage, size_sums.at[k - 1], "seq", peer) for k, peer in peers("seq")]
+    for copy in last:
+        copy.wait_recv()
     for k, _ in peers("seq"):
         size_total = size_total + size_sums[k - 1]
-    size_out[...] = size_total
-    for t in range(1, count):
-        for h in range(2):
-
-            @pl.when(rank <= t - 1)
-            def _():
-                link(True, t, h).wait_send()
-
-            @pl.when(count - 1 - rank <= t - 1)
-            def _():
-                link(False, t, h).wait_send()
-
-
-def finish_step(attended, gathered, dora, down, grad, grad_blocks):
-    count, data_devices = lax.axis_size("seq"), lax.axis_size("dp")
-    depth, (rows, width) = attended.shape[1], grad.shape
-    rank, own_cols = down.shape[1], grad_blocks.shape[2]
-    block_rows = depth // data_devices
+    size_out[...] = size_total / magnitude_ref[...]
+    for owner in range(count):
+
+        @pl.when(rank != owner)
+        def _():
+            for h in range(2):
+                link(owner, h, 0).wait_send()
+
+    wires.drain()
+
+
+def back(owner, lengths, text_gain, image_gain, key_value, image, gathered, dora, grad, ratio, magnitude):
+    count, devices = lax.axis_size("seq"), lax.axis_size("dp")
+    rows, width = grad.shape
+    rank, depth = dora.shape
+    text = key_value.shape[0]
+    own_cols = ratio.shape[1]
+    block_rows = depth // devices
     f32, bf16 = jnp.float32, jnp.bfloat16
-    halves = (rows, width // 2)
+    others, data_others = count - 1, devices - 1
+    wires = 4 * others + 4 * data_others
     return pl.pallas_call(
-        finish_kernel,
+        back_kernel,
         out_shape=[
             jax.ShapeDtypeStruct((rows, width), bf16),
-            jax.ShapeDtypeStruct((1, width), f32),
+            jax.ShapeDtypeStruct((rank, depth), f32),
             jax.ShapeDtypeStruct((rank, own_cols), f32),
-            jax.ShapeDtypeStruct((data_devices, block_rows, rank), f32),
+            jax.ShapeDtypeStruct((1, own_cols), f32),
         ],
-        in_specs=[VMEM] * 6,
+        in_specs=[SMEM] * 2 + [VMEM] * 9,
         out_specs=[VMEM] * 4,
         scratch_shapes=[
-            pltpu.VMEM((count, 2) + halves, bf16),
-        ]
-        + [pltpu.VMEM((count - 1, 2) + halves, bf16)] * 4
-        + [
+            pltpu.VMEM((text + count * rows, depth), bf16),
+            pltpu.VMEM((text + count * rows, depth), bf16),
+            pltpu.VMEM((count * rows, depth), bf16),
+            pltpu.VMEM((count, 2, rows, width // 2), bf16),
+            pltpu.VMEM((2, count, 2, rows, width // 2), bf16),
+            pltpu.VMEM((rows, rank), bf16),
             pltpu.VMEM((count, rows, rank), bf16),
-            pltpu.VMEM((count - 1, rows, rank), bf16),
-            pltpu.VMEM((count - 1, rows, rank), bf16),
-            pltpu.VMEM((data_devices, rank, own_cols), bf16),
-            pltpu.VMEM((data_devices - 1, rank, own_cols), bf16),
+            pltpu.VMEM((others, rows, rank), bf16),
+            pltpu.VMEM((others, rows, rank), bf16),
+            pltpu.VMEM((devices, rank, own_cols), bf16),
+            pltpu.VMEM((data_others, rank, own_cols), bf16),
             pltpu.VMEM((rank, own_cols), bf16),
-            pltpu.VMEM((count - 1, rank, own_cols), bf16),
-            pltpu.VMEM((data_devices, block_rows, rank), bf16),
-            pltpu.VMEM((data_devices - 1, block_rows, rank), bf16),
-            pltpu.VMEM((block_rows, rank), bf16),
-            pltpu.VMEM((data_devices, block_rows, rank), bf16),
-            pltpu.VMEM((1, width), f32),
-            pltpu.VMEM((data_devices - 1, 1, width), f32),
-            pltpu.VMEM((1, width), f32),
-            pltpu.VMEM((count - 1, 1, width), f32),
-        ]
-        + [pltpu.SemaphoreType.DMA((count - 1, 2))] * 4
-        + sems(count - 1) * 2
-        + sems(data_devices - 1)
-        + sems(count - 1)
-        + sems(data_devices - 1) * 2
-        + sems(data_devices - 1)
-        + sems(count - 1),
+            pltpu.VMEM((others, rank, own_cols), bf16),
+            pltpu.VMEM((devices, rank, block_rows), bf16),
+            pltpu.VMEM((data_others, rank, block_rows), bf16),
+            pltpu.VMEM((rank, block_rows), bf16),
+            pltpu.VMEM((devices, rank, block_rows), bf16),
+            pltpu.VMEM((devices, 1, own_cols), f32),
+            pltpu.VMEM((data_others, 1, own_cols), f32),
+            pltpu.VMEM((1, own_cols), f32),
+            pltpu.VMEM((others, 1, own_cols), f32),
+            pltpu.SemaphoreType.DMA((count * 2,)),
+            pltpu.SemaphoreType.DMA((count * 4,)),
+            pltpu.SemaphoreType.DMA((wires,)),
+            pltpu.SemaphoreType.DMA((wires,)),
+        ],
         compiler_params=pltpu.CompilerParams(
             collective_id=3, has_side_effects=True, vmem_limit_bytes=58 * 2**20
         ),
-    )(attended, gathered, dora, down, grad, grad_blocks)
+    )(owner, lengths, text_gain, image_gain, key_value, image, gathered, dora, grad, ratio, magnitude)
 
 
 def on_device(
@@ -788,8 +751,7 @@
     magnitude,
     grad_out,
 ):
-    data_rank = lax.axis_index("dp")
-    bf16, f32 = jnp.bfloat16, jnp.float32
+    down = dora_a.T
     image_all, key_value, gathered, ratio = front(
         prompt_owner_sample,
         enc_states,
@@ -801,30 +763,26 @@
         kv_weight.reshape(kv_weight.shape[0], -1),
         jnp.transpose(image_query_key_value[0], (1, 0, 2)),
         proj_weight,
-        dora_a.T,
+        down,
         dora_b,
         magnitude[None],
         text_scale,
         text_shift,
     )
-    ratio = ratio[0]
-    scaled_up = gathered[dora_a.shape[0] :]
-    diffusion_length = jnp.sum(jnp.where(prompt_owner_sample == data_rank, lengths, 0))
-    attended = attention(diffusion_length, text_key_gain, image_qk_gain, key_value, image_all)
-
-    down = lax.dot_general(
-        grad_out[0], scaled_up, (((1,), (1,)), ((), ())), preferred_element_type=f32
-    ).astype(bf16)
-    data_devices = lax.axis_size("dp")
-    grad_blocks = grad_out[0].reshape(grad_out.shape[1], data_devices, -1).transpose(1, 0, 2)
-    image_out, sizes, column_sums, grad_a = finish_step(
-        attended, gathered, dora_a.astype(bf16), down, grad_out[0], grad_blocks
+    image_out, grad_a, grad_b, grad_magnitude = back(
+        prompt_owner_sample,
+        lengths,
+        text_key_gain[None],
+        image_qk_gain,
+        key_value,
+        image_all,
+        gathered,
+        down,
+        grad_out[0],
+        ratio,
+        magnitude[None],
     )
-    grad_a = grad_a.reshape(-1, dora_b.shape[0])
-    grad_b = column_sums * ratio
-    own_cols = magnitude.shape[0]
-    grad_magnitude = lax.dynamic_slice_in_dim(sizes[0], data_rank * own_cols, own_cols, 0) / magnitude
-    return (image_out[None], grad_a, grad_b, grad_magnitude)
+    return (image_out[None], grad_a.T, grad_b, grad_magnitude[0])
 
 
 def solution(mesh):

time: 230 us -> 214 us (0.930)
  Pallas kernels: 213 us -> 203 us
  local copies, waits for them, and re-layouts: 11.4 us -> 8.95 us
    pallas_call x2 -> x1, Pallas kernels: 88.3 us -> 78.7 us  [back(): pl.pallas_call(back_kernel, out_shape=[jax.ShapeDtypeStruct((rows, width)...]
    unnamed x16 -> x4, local copies, waits for them, and re-layouts: 6.77 us -> 7.7 us
where the time goes in v1:
time: 214 us
  Pallas kernels  203 us (95%)
  local copies, waits for them, and re-layouts  8.95 us (4%)
    pallas_call x1, Pallas kernels, front(): pl.pallas_call(front_kernel, out_shape=[jax.ShapeDtypeStruct((count, kind...  124 us
    pallas_call x1, Pallas kernels, back(): pl.pallas_call(back_kernel, out_shape=[jax.ShapeDtypeStruct((rows, width)...  78.7 us
    unnamed x4, local copies, waits for them, and re-layouts  7.7 us

profile of v1, /device:TPU:0, one launch (start us, length us, event | category | flops | bytes accessed | tf_op | source)
XLA Modules:
  0.0 214.0 jit_solution(15798874774644954659)
XLA Ops:
  0.6 1.2 broadcast_in_dim.19.magnitude_ref
  1.9 2.5 %copy.23 = bf16[48,8,2,768]{3,1,2,0:T(8,128)(2,1)} copy(bf16[48,8,2,768]{3,2,1,0:T(2,128)(2,1)} %bitcast.14) | data formatting | bytes 2359296
  4.4 124.5 %shard_map.210 = (bf16[4,3,128,768]{3,2,1,0:T(8,128)(2,1)}, f32[128,1536]{1,0:T(8,128)}, bf16[832,3072]{1,0:T(8,128)(2,1)}, f32[1,384]{1,0:T(1,128)}) custom-call(s32[8]{0:T(128)} %owner_ref.3, bf16[1,256,4096]{2,1,0:T(8,128)(2,1)} %enc_ref.1, f32[1,4096]{1,0:T(1,128)} %bitcast.20, bf16[2,4096,1280]{2,1,0:T(8,128)(2,1)} %in_ref.1, ...), custom_call_target="tpu_custom_call" | custom-call | tf_op jit(solution)/shard_map/pallas_call | solution.py:412
  128.9 78.7 %shard_map.211 = (bf16[128,3072]{1,0:T(8,128)(2,1)}, f32[64,768]{1,0:T(8,128)}, f32[64,384]{1,0:T(8,128)}, f32[1,384]{1,0:T(1,128)}) custom-call(s32[8]{0:T(128)} %owner_ref.3, s32[8]{0:T(128)} %lengths_ref.1, f32[1,128]{1,0:T(1,128)} %bitcast.22, f32[2,128]{1,0:T(2,128)} %image_gain_ref.1, f32[128,1536]{1,0:T(8,128)} %get-tuple-element.12.key_value_ref, ...), custom_call_target="tpu_custom_call" | custom-call | tf_op jit(solution)/shard_map/pallas_call | solution.py:690
  207.5 1.3 reduce
  208.8 2.1 copy.27
  210.9 1.6 copy.28
  212.5 1.5 copy.29

commit v2 on v1

--- a/solution.py
+++ b/solution.py
@@ -157,14 +157,135 @@
     return next(t for t in (largest, largest // 2, 256, 128, width) if width % t == 0)
 
 
+class Chain:
+    def __init__(self, part, slot, send_sems, recv_sems, chunks):
+        self.part, self.slot, self.chunks = part, slot, chunks
+        self.send_sems, self.recv_sems = send_sems, recv_sems
+        self.count, self.rank = lax.axis_size("seq"), lax.axis_index("seq")
+        self.near = 1 - lax.div(self.rank, self.count // 2)
+        self.far = 1 - self.near
+
+    def target(self, step, right):
+        return right * (self.count - 1 - step) + (1 - right) * step
+
+    def link(self, owner, c, right):
+        return pltpu.make_async_remote_copy(
+            src_ref=self.part(owner, c),
+            dst_ref=self.slot(right, owner, c),
+            send_sem=self.send_sems.at[owner * self.chunks + c],
+            recv_sem=self.recv_sems.at[(right * self.count + owner) * self.chunks + c],
+            device_id={"seq": jnp.clip(self.rank + 2 * right - 1, 0, self.count - 1)},
+            device_id_type=MESH,
+        )
+
+    def begin(self, step, chunks=None):
+        owner = self.target(step, self.near)
+
+        @pl.when((self.rank == 0) | (self.rank == self.count - 1))
+        def _():
+            for c in range(self.chunks) if chunks is None else chunks:
+                self.link(owner, c, self.near).start()
+
+    def forward(self, step, right, chunks=None):
+        owner = self.target(step, right)
+        ahead = right * (owner - self.rank) + (1 - right) * (self.rank - owner)
+        behind = right * self.rank + (1 - right) * (self.count - 1 - self.rank)
+
+        @pl.when((ahead > 0) & (behind > 0))
+        def _():
+            for c in range(self.chunks) if chunks is None else chunks:
+                self.link(owner, c, right).wait_recv()
+                part = self.part(owner, c)
+                part[...] = (
+                    part[...].astype(jnp.float32) + self.slot(right, owner, c)[...].astype(jnp.float32)
+                ).astype(part.dtype)
+                self.link(owner, c, right).start()
+
+    def arrive(self, c):
+        @pl.when(self.rank >= 1)
+        def _():
+            self.link(self.rank, c, 1).wait_recv()
+
+        @pl.when(self.rank <= self.count - 2)
+        def _():
+            self.link(self.rank, c, 0).wait_recv()
+
+    def total(self, part, from_left, from_right):
+        total = part.astype(jnp.float32)
+        total = total + jnp.where(self.rank >= 1, from_left.astype(jnp.float32), 0.0)
+        return total + jnp.where(self.rank <= self.count - 2, from_right.astype(jnp.float32), 0.0)
+
+    def drain(self):
+        for owner in range(self.count):
+
+            @pl.when(self.rank != owner)
+            def _():
+                for c in range(self.chunks):
+                    self.link(owner, c, 0).wait_send()
+
+
+class Relay:
+    def __init__(self, block, send_sems, recv_sems):
+        self.block, self.send_sems, self.recv_sems = block, send_sems, recv_sems
+        self.count, self.rank = lax.axis_size("seq"), lax.axis_index("seq")
+
+    def link(self, owner, hop, right):
+        index = right * (self.count - 1) + hop
+        where = self.block(owner)
+        return pltpu.make_async_remote_copy(
+            src_ref=where,
+            dst_ref=where,
+            send_sem=self.send_sems.at[index],
+            recv_sem=self.recv_sems.at[index],
+            device_id={"seq": jnp.clip(self.rank + 2 * right - 1, 0, self.count - 1)},
+            device_id_type=MESH,
+        )
+
+    def reaches(self, right):
+        return self.rank < self.count - 1 if right else self.rank > 0
+
+    def begin(self):
+        for right in (1, 0):
+
+            @pl.when(self.reaches(right))
+            def _():
+                self.link(self.rank, 0, right).start()
+
+    def forward(self, hop):
+        for right in (1, 0):
+            owner = self.rank - hop if right else self.rank + hop
+            there = owner >= 0 if right else owner < self.count
+            owner = jnp.clip(owner, 0, self.count - 1)
+
+            @pl.when(there)
+            def _():
+                self.link(owner, hop - 1, right).wait_recv()
+
+            if hop < self.count - 1:
+
+                @pl.when(there & self.reaches(right))
+                def _():
+                    self.link(owner, hop, right).start()
+
+    def drain(self):
+        for hop in range(self.count - 1):
+            for right in (1, 0):
+                owner = self.rank - hop if right else self.rank + hop
+                there = owner >= 0 if right else owner < self.count
+
+                @pl.when(there & self.reaches(right))
+                def _():
+                    self.link(self.rank, hop, right).wait_send()
+
+
 def front_kernel(
     owner_ref, enc_ref, gain_ref, in_ref, out_ref, final_ref, context_ref, kv_ref, image_ref,
     proj_ref, down_ref, up_ref, magnitude_ref, scale_ref, shift_ref,
     image_all, key_value, gathered, ratio_ref,
     tokens, normed, in_tiles, out_all, hidden, part, sum_slots, encoded, context_all, kv_all,
-    context_part, row_slots, stage, prompts, sibling_prompts, final, text_all,
+    context_part, row_slots, stage, prompts, sibling_prompts, text_all,
     direction, squares, square_slots, own_scaled,
-    in_sems, local_sems, send_sems, recv_sems,
+    in_sems, local_sems, send_sems, recv_sems, sum_send, sum_recv, row_send, row_recv, text_send, text_recv,
 ):
     f32, bf16 = jnp.float32, jnp.bfloat16
     count, devices = lax.axis_size("seq"), lax.axis_size("dp")
@@ -214,17 +335,20 @@
     ]
     greet("seq", "dp")
     context_gather.first()
-    image_copies = [
-        wires.send(image_ref.at[:, :, heads_of(peer)], image_all.at[k], "seq", peer)
-        for k, peer in peers("seq")
-        if k != late
-    ]
-
-    def late_image(kind):
-        peer = lax.rem(rank + late, count)
-        image_copies.append(
-            wires.send(image_ref.at[kind, :, heads_of(peer)], image_all.at[late, kind], "seq", peer)
-        )
+    image_copies = []
+
+    def image(k, kind):
+        peer = lax.rem(rank + k, count)
+        image_copies.append(wires.send(image_ref.at[kind, :, heads_of(peer)], image_all.at[k, kind], "seq", peer))
+
+    def images(kinds):
+        for k in range(2, count):
+            if k != late:
+                for kind in kinds:
+                    image(k, kind)
+
+    for kind in range(3):
+        image(1, kind)
 
     for copy in locals_:
         copy.start()
@@ -252,20 +376,28 @@
 
     out_copy.wait()
     out_tile = tile_of(feat, 512)
-    sums = []
-    for k in [late] + [k for k in range(1, count) if k != late] + [0]:
-        owner = lax.rem(rank + k, count)
-        for t in range(0, feat, out_tile):
-            columns = pl.ds(pl.multiple_of(owner * feat + t, 128), out_tile)
-            part[k, :, t : t + out_tile] = jnp.dot(
+
+    def piece(c):
+        return slice(c * out_tile, (c + 1) * out_tile)
+
+    sums = Chain(
+        lambda owner, c: part.at[owner, :, piece(c)],
+        lambda right, owner, c: sum_slots.at[right, owner, :, piece(c)],
+        sum_send,
+        sum_recv,
+        feat // out_tile,
+    )
+    if late > 1:
+        image(late, 0)
+    for step in range(count):
+        owner = sums.target(step, sums.near)
+        for c in range(sums.chunks):
+            columns = pl.ds(pl.multiple_of(owner * feat + c * out_tile, 128), out_tile)
+            part[owner, :, piece(c)] = jnp.dot(
                 hidden[...], out_all[:, columns], preferred_element_type=f32
             ).astype(bf16)
-            if k:
-                sums.append(
-                    wires.send(
-                        part.at[k, :, t : t + out_tile], sum_slots.at[k - 1, :, t : t + out_tile], "seq", owner
-                    )
-                )
+            if step < count - 1:
+                sums.begin(step, (c,))
 
     context_gather.second()
     kv_gather.first()
@@ -284,40 +416,49 @@
     squares[...] = total
     square_copies = [wires.send(squares, square_slots.at[k - 1], "seq", peer) for k, peer in peers("seq")]
 
+    for step in range(count - 1):
+        sums.forward(step, sums.near)
+        sums.forward(step, sums.far)
     context_gather.third()
-    for copy in sums:
-        copy.wait_recv()
-    late_image(0)
+    for c in range(sums.chunks):
+        sums.arrive(c)
+    images((0,))
     own = pl.ds(pl.multiple_of(rank * feat, 128), feat)
     for r in range(0, text, 32):
-        total = part[0, r : r + 32, :].astype(f32)
-        for k in range(1, count):
-            total = total + sum_slots[k - 1, r : r + 32, :].astype(f32)
-        encoded[r : r + 32, :] = (
-            (tokens[r : r + 32, own].astype(f32) + total) * final_ref[:, own]
-        ).astype(bf16)
+        block = slice(r, r + 32)
+        total = sums.total(part[rank, block, :], sum_slots[1, rank, block, :], sum_slots[0, rank, block, :])
+        encoded[block, :] = ((tokens[block, own].astype(f32) + total) * final_ref[:, own]).astype(bf16)
 
     locals_[1].wait()
     context_gather.done()
-    if flat:
-        step = tile_of(width, 512)
-        for c in range(0, width, step):
-            context_part[:, c : c + step] = jnp.dot(
-                encoded[...], context_all[:, c : c + step], preferred_element_type=f32
-            ).astype(bf16)
-    else:
-        for d in range(devices):
-            context_part[:, d * own_cols : (d + 1) * own_cols] = jnp.dot(
-                encoded[...], context_all[d], preferred_element_type=f32
-            ).astype(bf16)
+    if late > 1:
+        image(late, 1)
 
     def block_of(index):
         return pl.ds(pl.multiple_of(index * rows, 16), rows)
 
-    row_copies = [
-        wires.send(context_part.at[block_of(peer)], row_slots.at[k - 1], "seq", peer) for k, peer in peers("seq")
-    ]
-    kv_gather.second()
+    half = width // 2
+    row_sums = Chain(
+        lambda owner, c: context_part.at[block_of(owner), c * half : (c + 1) * half],
+        lambda right, owner, c: row_slots.at[right, owner, :, c * half : (c + 1) * half],
+        row_send,
+        row_recv,
+        2,
+    )
+    for c in range(2):
+        if flat:
+            step = tile_of(half, 512)
+            for start in range(c * half, (c + 1) * half, step):
+                context_part[:, start : start + step] = jnp.dot(
+                    encoded[...], context_all[:, start : start + step], preferred_element_type=f32
+                ).astype(bf16)
+        else:
+            for d in range(c * devices // 2, (c + 1) * devices // 2):
+                context_part[:, d * own_cols : (d + 1) * own_cols] = jnp.dot(
+                    encoded[...], context_all[d], preferred_element_type=f32
+                ).astype(bf16)
+        for step in range(count - 1):
+            row_sums.begin(step, (c,))
     for copy in square_copies:
         copy.wait_recv()
     total = squares[...]
@@ -329,12 +470,15 @@
         own_scaled[r : r + 128, :] = (direction[r : r + 128, :] * ratio).astype(bf16)
     own_scaled[depth:, :] = (up_ref[...] * ratio).astype(bf16)
 
-    for copy in row_copies:
-        copy.wait_recv()
-    total = context_part[block_of(rank), :].astype(f32)
-    for k in range(1, count):
-        total = total + row_slots[k - 1].astype(f32)
-    stage[...] = total.astype(bf16)
+    for c in range(2):
+        for step in range(count - 1):
+            row_sums.forward(step, row_sums.near, (c,))
+            row_sums.forward(step, row_sums.far, (c,))
+    for c in range(2):
+        row_sums.arrive(c)
+    stage[...] = row_sums.total(
+        context_part[block_of(rank), :], row_slots[1, rank], row_slots[0, rank]
+    ).astype(bf16)
 
     chips = devices // 2
     chip = lax.div(data_rank, 2)
@@ -344,10 +488,10 @@
         for j in range(1, chips)
     ]
     shared = [wires.send(stage, sibling_prompts.at[0], "dp", sibling)]
-    scaled_gather.first()
+    images((1, 2))
+    kv_gather.second()
     local_scaled = local(own_scaled, scaled_view(gathered, data_rank, None), 5)
     local_scaled.start()
-    late_image(1)
     for j in range(1, chips):
         prompt_copies[j - 1].wait_recv()
         shared.append(wires.send(prompts.at[j - 1], sibling_prompts.at[j], "dp", sibling))
@@ -362,34 +506,39 @@
     centre = jnp.mean(routed, -1, keepdims=True)
     spread = jnp.mean((routed - centre) * (routed - centre), -1, keepdims=True)
     layer_normed = (routed - centre) * lax.rsqrt(spread + EPSILON)
-    final[...] = ((1.0 + scale_ref[...]) * layer_normed + shift_ref[...]).astype(bf16)
-    text_copies = [wires.send(final, text_all.at[block_of(rank)], "seq", peer) for _, peer in peers("seq")]
-    text_all[block_of(rank), :] = final[...]
-    late_image(2)
+    text_all[block_of(rank), :] = ((1.0 + scale_ref[...]) * layer_normed + shift_ref[...]).astype(bf16)
+    scaled_gather.first()
+    if late > 1:
+        image(late, 2)
+    texts = Relay(lambda owner: text_all.at[block_of(owner)], text_send, text_recv)
+    texts.begin()
+    for hop in range(1, count):
+        texts.forward(hop)
     kv_gather.third()
-    scaled_gather.second()
     locals_[2].wait()
     kv_gather.done()
-    for copy in text_copies:
-        copy.wait_recv()
     step = tile_of(kv_all.shape[1], 512)
     for c in range(0, kv_all.shape[1], step):
         key_value[:, c : c + step] = jnp.dot(
             text_all[...], kv_all[:, c : c + step], preferred_element_type=f32
         )
+    scaled_gather.second()
     scaled_gather.third()
     locals_[0].wait()
     local_scaled.wait()
     for copy in image_copies:
         copy.wait_recv()
     scaled_gather.done()
+    sums.drain()
+    row_sums.drain()
+    texts.drain()
     wires.drain()
 
 
-def wires_needed(count, pairs, sum_tiles):
+def wires_needed(count, pairs):
     others = count - 1
     gathers = 3 * (pairs + 4 * (pairs - 1) + pairs + 2)
-    return others + 3 + others * (sum_tiles + 3) + 4 * pairs + gathers
+    return 4 * others + 4 * pairs + gathers
 
 
 def front(owner, enc, gain, w_in, w_out, final_gain, context, kv, image, proj, down, up, magnitude, scale, shift):
@@ -406,7 +555,8 @@
     scaled_rows = proj.shape[0] + up.shape[0]
     tile = tile_of(hidden, 256)
     slots = 3
-    wires = wires_needed(count, devices // 4, feat // tile_of(feat, 512))
+    pieces = feat // tile_of(feat, 512)
+    wires = wires_needed(count, devices // 4)
     any_ = pl.BlockSpec(memory_space=pl.ANY)
     gathered_shape = column_shape(devices, scaled_rows, own_cols)
     outs = pl.pallas_call(
@@ -426,16 +576,15 @@
             pltpu.VMEM((hidden, width_enc), bf16),
             pltpu.VMEM((text, hidden), bf16),
             pltpu.VMEM((count, text, feat), bf16),
-            pltpu.VMEM((count - 1, text, feat), bf16),
+            pltpu.VMEM((2, count, text, feat), bf16),
             pltpu.VMEM((text, feat), bf16),
             pltpu.VMEM(column_shape(devices, context.shape[0], own_cols), bf16),
             pltpu.VMEM((kv.shape[0] * devices, kv.shape[1]), bf16),
             pltpu.VMEM((text, width), bf16),
-            pltpu.VMEM((count - 1, rows, width), bf16),
+            pltpu.VMEM((2, count, rows, width), bf16),
             pltpu.VMEM((rows, width), bf16),
             pltpu.VMEM((devices // 2 - 1, rows, width), bf16),
             pltpu.VMEM((devices // 2, rows, width), bf16),
-            pltpu.VMEM((rows, width), bf16),
             pltpu.VMEM((text, width), bf16),
             pltpu.VMEM(proj.shape, f32),
             pltpu.VMEM((1, own_cols), f32),
@@ -445,6 +594,12 @@
             pltpu.SemaphoreType.DMA((6,)),
             pltpu.SemaphoreType.DMA((wires,)),
             pltpu.SemaphoreType.DMA((wires,)),
+            pltpu.SemaphoreType.DMA((count * pieces,)),
+            pltpu.SemaphoreType.DMA((count * 2 * pieces,)),
+            pltpu.SemaphoreType.DMA((count * 2,)),
+            pltpu.SemaphoreType.DMA((count * 4,)),
+            pltpu.SemaphoreType.DMA((count * 2,)),
+            pltpu.SemaphoreType.DMA((count * 2,)),
         ],
         compiler_params=pltpu.CompilerParams(
             collective_id=1, has_side_effects=True, vmem_limit_bytes=62 * 2**20
@@ -478,44 +633,18 @@
     over_rows = (((0,), (0,)), ((), ()))
     over_columns = (((1,), (1,)), ((), ()))
     wires = Wires(send_sems, recv_sems)
-    near = 1 - lax.div(rank, count // 2)
-
-    def target_of(step, right):
-        return right * (count - 1 - step) + (1 - right) * step
 
     def block_of(owner):
         return lax.rem(rank + count - owner, count)
 
-    def link(owner, h, right):
-        index = (right * count + owner) * 2 + h
-        return pltpu.make_async_remote_copy(
-            src_ref=parts.at[owner, h],
-            dst_ref=slots.at[right, owner, h],
-            send_sem=chain_send.at[owner * 2 + h],
-            recv_sem=chain_recv.at[index],
-            device_id={"seq": jnp.clip(rank + 2 * right - 1, 0, count - 1)},
-            device_id_type=MESH,
-        )
-
-    def begin(step):
-        owner = target_of(step, near)
-
-        @pl.when((rank == 0) | (rank == count - 1))
-        def _():
-            for h in range(2):
-                link(owner, h, near).start()
-
-    def forward(step, right):
-        owner = target_of(step, right)
-        ahead = right * (owner - rank) + (1 - right) * (rank - owner)
-        behind = right * rank + (1 - right) * (count - 1 - rank)
-
-        @pl.when((ahead > 0) & (behind > 0))
-        def _():
-            for h in range(2):
-                link(owner, h, right).wait_recv()
-                parts[owner, h] = (parts[owner, h].astype(f32) + slots[right, owner, h].astype(f32)).astype(bf16)
-                link(owner, h, right).start()
+    chain = Chain(
+        lambda owner, h: parts.at[owner, h],
+        lambda right, owner, h: slots.at[right, owner, h],
+        chain_send,
+        chain_recv,
+        2,
+    )
+    near, far = chain.near, chain.far
 
     greet("seq", "dp")
     down[...] = lax.dot_general(
@@ -549,7 +678,7 @@
     scale = 1.0 / math.sqrt(HD)
 
     for step in range(count):
-        owner = target_of(step, near)
+        owner = chain.target(step, near)
         block = block_of(owner)
         block_slice = pl.ds(pl.multiple_of(block * rows, 16), rows)
 
@@ -572,7 +701,7 @@
                 attended[block_slice, :], weight_ref[:depth, columns], preferred_element_type=f32
             ).astype(bf16)
         if step == 0:
-            begin(0)
+            chain.begin(0)
 
     dora = dora_ref[...].astype(bf16)
     ups = lax.dot_general(attended[...], dora, over_columns, preferred_element_type=f32).astype(bf16)
@@ -582,8 +711,8 @@
         before = lax.rem(rank + count - k, count)
         small.append(wires.send(up.at[k], up_slots.at[k - 1], "seq", before))
     for step in range(1, count - 2):
-        begin(step)
-    forward(0, near)
+        chain.begin(step)
+    chain.forward(0, near)
     for copy in small:
         copy.wait_recv()
     up_total = up[0].astype(f32)
@@ -619,27 +748,17 @@
     for k, peer in peers("dp"):
         second.append(wires.send(row_stage, row_sums.at[data_rank], "dp", peer))
     row_sums[data_rank] = row_stage[...]
-    begin(count - 2)
-    forward(0, 1 - near)
+    chain.begin(count - 2)
+    chain.forward(0, far)
     for step in range(1, count - 1):
-        forward(step, near)
-        forward(step, 1 - near)
+        chain.forward(step, near)
+        chain.forward(step, far)
 
     sums = []
     for h in range(2):
-
-        @pl.when(rank >= 1)
-        def _():
-            link(rank, h, 1).wait_recv()
-
-        @pl.when(rank <= count - 2)
-        def _():
-            link(rank, h, 0).wait_recv()
-
+        chain.arrive(h)
         columns = slice(h * half, (h + 1) * half)
-        total = parts[rank, h].astype(f32)
-        total = total + jnp.where(rank >= 1, slots[1, rank, h].astype(f32), 0.0)
-        total = total + jnp.where(rank <= count - 2, slots[0, rank, h].astype(f32), 0.0)
+        total = chain.total(parts[rank, h], slots[1, rank, h], slots[0, rank, h])
         image_out[:, columns] = total.astype(bf16)
         sums.append(jnp.sum(grad_ref[:, columns].astype(f32) * total, 0, keepdims=True))
     per_half = devices // 2
@@ -667,13 +786,7 @@
     for k, _ in peers("seq"):
         size_total = size_total + size_sums[k - 1]
     size_out[...] = size_total / magnitude_ref[...]
-    for owner in range(count):
-
-        @pl.when(rank != owner)
-        def _():
-            for h in range(2):
-                link(owner, h, 0).wait_send()
-
+    chain.drain()
     wires.drain()
 
 

time: 214 us -> 216 us (level)
    pallas_call x1, Pallas kernels: 124 us -> 128 us  [front(): pl.pallas_call(front_kernel, out_shape=[jax.ShapeDtypeStruct((count, kind...]
where the time goes in v2:
time: 216 us
  Pallas kernels  205 us (95%)
  local copies, waits for them, and re-layouts  8.95 us (4%)
    pallas_call x1, Pallas kernels, front(): pl.pallas_call(front_kernel, out_shape=[jax.ShapeDtypeStruct((count, kind...  128 us
    pallas_call x1, Pallas kernels, back(): pl.pallas_call(back_kernel, out_shape=[jax.ShapeDtypeStruct((rows, width)...  77.1 us
    unnamed x4, local copies, waits for them, and re-layouts  7.7 us

profile of v2, /device:TPU:0, one launch (start us, length us, event | category | flops | bytes accessed | tf_op | source)
XLA Modules:
  0.0 216.1 jit_solution(15141341829161054712)
XLA Ops:
  0.6 1.2 broadcast_in_dim.19.magnitude_ref
  1.9 2.5 %copy.23 = bf16[48,8,2,768]{3,1,2,0:T(8,128)(2,1)} copy(bf16[48,8,2,768]{3,2,1,0:T(2,128)(2,1)} %bitcast.14) | data formatting | bytes 2359296
  4.4 128.1 %shard_map.210 = (bf16[4,3,128,768]{3,2,1,0:T(8,128)(2,1)}, f32[128,1536]{1,0:T(8,128)}, bf16[832,3072]{1,0:T(8,128)(2,1)}, f32[1,384]{1,0:T(1,128)}) custom-call(s32[8]{0:T(128)} %owner_ref.3, bf16[1,256,4096]{2,1,0:T(8,128)(2,1)} %enc_ref.1, f32[1,4096]{1,0:T(1,128)} %bitcast.20, bf16[2,4096,1280]{2,1,0:T(8,128)(2,1)} %in_ref.1, ...), custom_call_target="tpu_custom_call" | custom-call | tf_op jit(solution)/shard_map/pallas_call | solution.py:562
  132.5 77.1 %shard_map.211 = (bf16[128,3072]{1,0:T(8,128)(2,1)}, f32[64,768]{1,0:T(8,128)}, f32[64,384]{1,0:T(8,128)}, f32[1,384]{1,0:T(1,128)}) custom-call(s32[8]{0:T(128)} %owner_ref.3, s32[8]{0:T(128)} %lengths_ref.1, f32[1,128]{1,0:T(1,128)} %bitcast.22, f32[2,128]{1,0:T(2,128)} %image_gain_ref.1, f32[128,1536]{1,0:T(8,128)} %get-tuple-element.12.key_value_ref, ...), custom_call_target="tpu_custom_call" | custom-call | tf_op jit(solution)/shard_map/pallas_call | solution.py:803
  209.6 1.3 reduce
  210.9 2.1 copy.27
  213.0 1.6 copy.28
  214.6 1.5 copy.29

commit v3 on v2

--- a/solution.py
+++ b/solution.py
@@ -1,3 +1,4 @@
+import functools
 import math
 
 import jax
@@ -157,6 +158,28 @@
     return next(t for t in (largest, largest // 2, 256, 128, width) if width % t == 0)
 
 
+def exp_scores(queries, keys):
+    scores = lax.dot_general(queries, keys, (((1,), (1,)), ((), ())), preferred_element_type=jnp.float32)
+    return jnp.exp(scores * (1.0 / math.sqrt(HD)))
+
+
+def pieces_of(own_cols):
+    return own_cols // 128 if flat_columns(own_cols) else 1
+
+
+def scaled_pieces(scaled, up_weight, weight, own_cols):
+    adapter = up_weight.shape[-2]
+    depth = scaled.shape[0] - adapter
+    pieces = pieces_of(own_cols)
+    piece = own_cols // pieces
+    flat = flat_columns(own_cols)
+    triples = [(scaled.at[pl.ds(depth, adapter)], up_weight, by_columns(adapter, own_cols, flat))]
+    for p in range(pieces):
+        source = scaled.at[pl.ds(0, depth), pl.ds(p * piece, piece)]
+        triples.append((source, weight.at[p], by_columns(depth, piece, flat)))
+    return triples
+
+
 class Chain:
     def __init__(self, part, slot, send_sems, recv_sems, chunks):
         self.part, self.slot, self.chunks = part, slot, chunks
@@ -278,14 +301,14 @@
                     self.link(self.rank, hop, right).wait_send()
 
 
-def front_kernel(
+def front_part(
     owner_ref, enc_ref, gain_ref, in_ref, out_ref, final_ref, context_ref, kv_ref, image_ref,
-    proj_ref, down_ref, up_ref, magnitude_ref, scale_ref, shift_ref,
-    image_all, key_value, gathered, ratio_ref,
-    tokens, normed, in_tiles, out_all, hidden, part, sum_slots, encoded, context_all, kv_all,
+    proj_ref, down_ref, up_ref, magnitude_ref, scale_ref, shift_ref, image_gain_ref,
+    queries, mixture, denominator, key_value, own_scaled, weight, up_weight, ratio_ref,
+    image_all, tokens, normed, in_tiles, out_tiles, hidden, part, sum_slots, encoded, context_all, kv_all,
     context_part, row_slots, stage, prompts, sibling_prompts, text_all,
-    direction, squares, square_slots, own_scaled,
-    in_sems, local_sems, send_sems, recv_sems, sum_send, sum_recv, row_send, row_recv, text_send, text_recv,
+    direction, squares, square_slots,
+    in_sems, out_sems, local_sems, send_sems, recv_sems, sum_send, sum_recv, row_send, row_recv, text_send, text_recv,
 ):
     f32, bf16 = jnp.float32, jnp.bfloat16
     count, devices = lax.axis_size("seq"), lax.axis_size("dp")
@@ -296,16 +319,43 @@
     feat = encoded.shape[1]
     width = context_part.shape[1]
     rows = stage.shape[0]
-    slots, _, _, tile = in_tiles.shape
+    slots = in_tiles.shape[0]
+    tile = in_tiles.shape[2] // 2
     tiles = hidden.shape[1] // tile
     depth, own_cols = proj_ref.shape
     flat = flat_columns(own_cols)
     late = count // 2
 
-    def in_copy(i, slot):
-        return pltpu.make_async_copy(
-            in_ref.at[:, :, pl.ds(pl.multiple_of(i * tile, 128), tile)], in_tiles.at[slot], in_sems.at[slot]
-        )
+    class in_copy:
+        def __init__(self, i, slot):
+            columns = pl.ds(pl.multiple_of(i * tile, 128), tile)
+            self.copies = [
+                pltpu.make_async_copy(
+                    in_ref.at[side, :, columns],
+                    in_tiles.at[slot, :, side * tile : (side + 1) * tile],
+                    in_sems.at[slot * 2 + side],
+                )
+                for side in range(2)
+            ]
+
+        def start(self):
+            for copy in self.copies:
+                copy.start()
+
+        def wait(self):
+            for copy in self.copies:
+                copy.wait()
+
+    near = 1 - lax.div(rank, count // 2)
+    out_slots, _, out_tile = out_tiles.shape
+    chunks = feat // out_tile
+
+    def out_copy(i):
+        step, c = divmod(i, chunks)
+        owner = near * (count - 1 - step) + (1 - near) * step
+        columns = pl.ds(pl.multiple_of(owner * feat + c * out_tile, 128), out_tile)
+        slot = i % out_slots
+        return pltpu.make_async_copy(out_ref.at[:, columns], out_tiles.at[slot], out_sems.at[slot])
 
     def local(source, target, index):
         return pltpu.make_async_copy(source, target, local_sems.at[index])
@@ -314,32 +364,67 @@
     token_copy.start()
     for i in range(min(slots, tiles)):
         in_copy(i, i).start()
-    out_copy = local(out_ref, out_all, 1)
-    out_copy.start()
+    for i in range(min(out_slots, count * chunks)):
+        out_copy(i).start()
 
     def heads_of(owner):
         head_width = image_all.shape[3]
         return pl.ds(pl.multiple_of(owner * head_width, 128), head_width)
 
     context_view = by_columns(context_ref.shape[0], own_cols, flat)
-    scaled_view = by_columns(own_scaled.shape[0], own_cols, flat)
     kv_view = by_rows(kv_ref.shape[0])
     context_gather = Gather(wires, place, context_ref, context_all, context_view)
     kv_gather = Gather(wires, place, kv_ref, kv_all, kv_view)
-    scaled_gather = Gather(wires, place, own_scaled, gathered, scaled_view)
 
     locals_ = [
         local(image_ref.at[:, :, heads_of(rank)], image_all.at[0], 2),
         local(context_ref, context_view(context_all, data_rank, None), 3),
         local(kv_ref, kv_view(kv_all, data_rank, None), 4),
     ]
+    scaled_gathers, scaled_locals = [], []
+    for source, target, view in scaled_pieces(own_scaled, up_weight, weight, own_cols)[:2]:
+        scaled_gathers.append(Gather(wires, place, source, target, view))
+        scaled_locals.append(local(source, view(target, data_rank, None), 5 + len(scaled_locals)))
+    image_rows = image_all.shape[2]
+    heads = image_all.shape[3] // HD
+
+    def head(h):
+        return pl.ds(pl.multiple_of(h * HD, HD), HD)
+
+    def query_step(h, carry):
+        for k in range(count):
+            queries[k * image_rows : (k + 1) * image_rows, head(h)] = rms_scale(
+                image_all[k, 0, :, head(h)].astype(f32), image_gain_ref[0:1, :]
+            ).astype(bf16)
+        return carry
+
+    def attend(k):
+        def head_step(h, carry):
+            keys = rms_scale(image_all[k, 1, :, head(h)].astype(f32), image_gain_ref[1:2, :]).astype(bf16)
+            share = exp_scores(queries[:, head(h)], keys)
+            total = jnp.broadcast_to(jnp.sum(share, -1, keepdims=True), (share.shape[0], HD))
+            mixed = jnp.dot(share.astype(bf16), image_all[k, 2, :, head(h)], preferred_element_type=f32)
+            if k:
+                total = total + denominator[:, head(h)]
+                mixed = mixed + mixture[:, head(h)]
+            denominator[:, head(h)] = total
+            mixture[:, head(h)] = mixed
+            return carry
+
+        if k:
+            image_copies[k, 1].wait_recv()
+            image_copies[k, 2].wait_recv()
+        lax.fori_loop(0, heads, head_step, 0)
+
     greet("seq", "dp")
     context_gather.first()
-    image_copies = []
+    image_copies = {}
 
     def image(k, kind):
         peer = lax.rem(rank + k, count)
-        image_copies.append(wires.send(image_ref.at[kind, :, heads_of(peer)], image_all.at[k, kind], "seq", peer))
+        image_copies[k, kind] = wires.send(
+            image_ref.at[kind, :, heads_of(peer)], image_all.at[k, kind], "seq", peer
+        )
 
     def images(kinds):
         for k in range(2, count):
@@ -361,8 +446,8 @@
     def in_step(i, carry):
         slot = lax.rem(i, slots)
         in_copy(i, slot).wait()
-        gate = jnp.dot(normed[...], in_tiles[slot, 0], preferred_element_type=f32)
-        upward = jnp.dot(normed[...], in_tiles[slot, 1], preferred_element_type=f32)
+        both = jnp.dot(normed[...], in_tiles[slot], preferred_element_type=f32)
+        gate, upward = both[:, :tile], both[:, tile:]
         columns = pl.ds(pl.multiple_of(i * tile, 128), tile)
         hidden[:, columns] = (jax.nn.gelu(gate, approximate=True) * upward).astype(bf16)
 
@@ -374,28 +459,28 @@
 
     lax.fori_loop(0, tiles, in_step, 0)
 
-    out_copy.wait()
-    out_tile = tile_of(feat, 512)
-
     def piece(c):
         return slice(c * out_tile, (c + 1) * out_tile)
 
     sums = Chain(
         lambda owner, c: part.at[owner, :, piece(c)],
-        lambda right, owner, c: sum_slots.at[right, owner, :, piece(c)],
+        lambda right, owner, c: sum_slots.at[owner + right, :, piece(c)],
         sum_send,
         sum_recv,
-        feat // out_tile,
+        chunks,
     )
     if late > 1:
         image(late, 0)
     for step in range(count):
         owner = sums.target(step, sums.near)
         for c in range(sums.chunks):
-            columns = pl.ds(pl.multiple_of(owner * feat + c * out_tile, 128), out_tile)
+            index = step * chunks + c
+            out_copy(index).wait()
             part[owner, :, piece(c)] = jnp.dot(
-                hidden[...], out_all[:, columns], preferred_element_type=f32
+                hidden[...], out_tiles[index % out_slots], preferred_element_type=f32
             ).astype(bf16)
+            if index + out_slots < count * chunks:
+                out_copy(index + out_slots).start()
             if step < count - 1:
                 sums.begin(step, (c,))
 
@@ -426,7 +511,7 @@
     own = pl.ds(pl.multiple_of(rank * feat, 128), feat)
     for r in range(0, text, 32):
         block = slice(r, r + 32)
-        total = sums.total(part[rank, block, :], sum_slots[1, rank, block, :], sum_slots[0, rank, block, :])
+        total = sums.total(part[rank, block, :], sum_slots[rank + 1, block, :], sum_slots[rank, block, :])
         encoded[block, :] = ((tokens[block, own].astype(f32) + total) * final_ref[:, own]).astype(bf16)
 
     locals_[1].wait()
@@ -440,7 +525,7 @@
     half = width // 2
     row_sums = Chain(
         lambda owner, c: context_part.at[block_of(owner), c * half : (c + 1) * half],
-        lambda right, owner, c: row_slots.at[right, owner, :, c * half : (c + 1) * half],
+        lambda right, owner, c: row_slots.at[owner + right, :, c * half : (c + 1) * half],
         row_send,
         row_recv,
         2,
@@ -459,6 +544,7 @@
                 ).astype(bf16)
         for step in range(count - 1):
             row_sums.begin(step, (c,))
+    kv_gather.second()
     for copy in square_copies:
         copy.wait_recv()
     total = squares[...]
@@ -477,7 +563,7 @@
     for c in range(2):
         row_sums.arrive(c)
     stage[...] = row_sums.total(
-        context_part[block_of(rank), :], row_slots[1, rank], row_slots[0, rank]
+        context_part[block_of(rank), :], row_slots[rank + 1], row_slots[rank]
     ).astype(bf16)
 
     chips = devices // 2
@@ -489,9 +575,15 @@
     ]
     shared = [wires.send(stage, sibling_prompts.at[0], "dp", sibling)]
     images((1, 2))
-    kv_gather.second()
-    local_scaled = local(own_scaled, scaled_view(gathered, data_rank, None), 5)
-    local_scaled.start()
+    for gather, copy in zip(scaled_gathers, scaled_locals):
+        gather.first()
+        copy.start()
+    locals_[0].wait()
+    for k in range(1, count):
+        image_copies[k, 0].wait_recv()
+    lax.fori_loop(0, heads, query_step, 0)
+    attend(0)
+    attend(1)
     for j in range(1, chips):
         prompt_copies[j - 1].wait_recv()
         shared.append(wires.send(prompts.at[j - 1], sibling_prompts.at[j], "dp", sibling))
@@ -507,14 +599,19 @@
     spread = jnp.mean((routed - centre) * (routed - centre), -1, keepdims=True)
     layer_normed = (routed - centre) * lax.rsqrt(spread + EPSILON)
     text_all[block_of(rank), :] = ((1.0 + scale_ref[...]) * layer_normed + shift_ref[...]).astype(bf16)
-    scaled_gather.first()
     if late > 1:
         image(late, 2)
     texts = Relay(lambda owner: text_all.at[block_of(owner)], text_send, text_recv)
     texts.begin()
+    for k in [k for k in range(2, count) if k != late] + [late] * (late > 1):
+        attend(k)
+    for gather in scaled_gathers:
+        gather.second()
     for hop in range(1, count):
         texts.forward(hop)
     kv_gather.third()
+    for gather in scaled_gathers:
+        gather.third()
     locals_[2].wait()
     kv_gather.done()
     step = tile_of(kv_all.shape[1], 512)
@@ -522,197 +619,127 @@
         key_value[:, c : c + step] = jnp.dot(
             text_all[...], kv_all[:, c : c + step], preferred_element_type=f32
         )
-    scaled_gather.second()
-    scaled_gather.third()
-    locals_[0].wait()
-    local_scaled.wait()
-    for copy in image_copies:
-        copy.wait_recv()
-    scaled_gather.done()
-    sums.drain()
-    row_sums.drain()
-    texts.drain()
-    wires.drain()
-
-
-def wires_needed(count, pairs):
-    others = count - 1
-    gathers = 3 * (pairs + 4 * (pairs - 1) + pairs + 2)
-    return 4 * others + 4 * pairs + gathers
-
-
-def front(owner, enc, gain, w_in, w_out, final_gain, context, kv, image, proj, down, up, magnitude, scale, shift):
-    count, devices = lax.axis_size("seq"), lax.axis_size("dp")
-    bf16, f32 = jnp.bfloat16, jnp.float32
-    width_enc, hidden = w_in.shape[1:]
-    feat = width_enc // count
-    text = MAX_PROMPT
-    width = scale.shape[1]
-    rows = text // count
-    kinds, image_rows, _ = image.shape
-    head_width = width // count
-    own_cols = proj.shape[1]
-    scaled_rows = proj.shape[0] + up.shape[0]
-    tile = tile_of(hidden, 256)
-    slots = 3
-    pieces = feat // tile_of(feat, 512)
-    wires = wires_needed(count, devices // 4)
-    any_ = pl.BlockSpec(memory_space=pl.ANY)
-    gathered_shape = column_shape(devices, scaled_rows, own_cols)
-    outs = pl.pallas_call(
-        front_kernel,
-        out_shape=[
-            jax.ShapeDtypeStruct((count, kinds, image_rows, head_width), bf16),
-            jax.ShapeDtypeStruct((text, kv.shape[1]), f32),
-            jax.ShapeDtypeStruct(gathered_shape, bf16),
-            jax.ShapeDtypeStruct((1, own_cols), f32),
-        ],
-        in_specs=[SMEM, any_, VMEM, any_, any_, VMEM, any_, any_, any_] + [VMEM] * 6,
-        out_specs=[VMEM] * 4,
-        scratch_shapes=[
-            pltpu.VMEM((text, width_enc), bf16),
-            pltpu.VMEM((text, width_enc), bf16),
-            pltpu.VMEM((slots, 2, width_enc, tile), bf16),
-            pltpu.VMEM((hidden, width_enc), bf16),
-            pltpu.VMEM((text, hidden), bf16),
-            pltpu.VMEM((count, text, feat), bf16),
-            pltpu.VMEM((2, count, text, feat), bf16),
-            pltpu.VMEM((text, feat), bf16),
-            pltpu.VMEM(column_shape(devices, context.shape[0], own_cols), bf16),
-            pltpu.VMEM((kv.shape[0] * devices, kv.shape[1]), bf16),
-            pltpu.VMEM((text, width), bf16),
-            pltpu.VMEM((2, count, rows, width), bf16),
-            pltpu.VMEM((rows, width), bf16),
-            pltpu.VMEM((devices // 2 - 1, rows, width), bf16),
-            pltpu.VMEM((devices // 2, rows, width), bf16),
-            pltpu.VMEM((text, width), bf16),
-            pltpu.VMEM(proj.shape, f32),
-            pltpu.VMEM((1, own_cols), f32),
-            pltpu.VMEM((count - 1, 1, own_cols), f32),
-            pltpu.VMEM((scaled_rows, own_cols), bf16),
-            pltpu.SemaphoreType.DMA((slots,)),
-            pltpu.SemaphoreType.DMA((6,)),
-            pltpu.SemaphoreType.DMA((wires,)),
-            pltpu.SemaphoreType.DMA((wires,)),
-            pltpu.SemaphoreType.DMA((count * pieces,)),
-            pltpu.SemaphoreType.DMA((count * 2 * pieces,)),
-            pltpu.SemaphoreType.DMA((count * 2,)),
-            pltpu.SemaphoreType.DMA((count * 4,)),
-            pltpu.SemaphoreType.DMA((count * 2,)),
-            pltpu.SemaphoreType.DMA((count * 2,)),
-        ],
-        compiler_params=pltpu.CompilerParams(
-            collective_id=1, has_side_effects=True, vmem_limit_bytes=62 * 2**20
-        ),
-    )(owner, enc, gain, w_in, w_out, final_gain, context, kv, image, proj, down, up, magnitude, scale, shift)
-    image_all, key_value, gathered, ratio = outs
-    if not flat_columns(own_cols):
-        gathered = gathered.transpose(1, 0, 2).reshape(scaled_rows, -1)
-    return image_all, key_value, gathered, ratio
-
-
-def back_kernel(
-    owner_ref, lengths_ref, text_gain_ref, image_gain_ref, key_value_ref, image_ref, weight_ref, dora_ref,
-    grad_ref, ratio_ref, magnitude_ref,
+    for gather, copy in zip(scaled_gathers, scaled_locals):
+        gather.done()
+        copy.wait()
+    return sums, row_sums, texts, wires
+
+
+def back_part(
+    owner_ref, lengths_ref, text_gain_ref, key_value_ref, queries_ref, mixture_ref, denominator_ref,
+    scaled_ref, weight, up_weight_ref, dora_ref, grad_ref, ratio_ref, magnitude_ref,
     image_out, down_out, cols_out, size_out,
-    keys, values, attended, parts, slots, down, up, up_slots, down_slots,
+    attended, parts, slots, down, up, up_slots, down_slots,
     cols, col_slots, col_stage, col_sums, rows_all, row_slots, row_stage, row_sums,
     size, size_slots, size_stage, size_sums,
-    chain_send, chain_recv, send_sems, recv_sems,
+    local_sems, chain_send, chain_recv, send_sems, recv_sems,
 ):
     count, devices = lax.axis_size("seq"), lax.axis_size("dp")
     rank, data_rank = lax.axis_index("seq"), lax.axis_index("dp")
     rows, width = image_out.shape
-    depth = image_ref.shape[3]
+    depth = queries_ref.shape[1]
     text = key_value_ref.shape[0]
     heads = depth // HD
-    half = width // 2
     own_cols = ratio_ref.shape[1]
+    adapter = dora_ref.shape[0]
+    pieces = pieces_of(own_cols)
+    piece = own_cols // pieces
+    flat = flat_columns(own_cols)
     block_rows = depth // devices
     f32, bf16 = jnp.float32, jnp.bfloat16
     over_rows = (((0,), (0,)), ((), ()))
     over_columns = (((1,), (1,)), ((), ()))
     wires = Wires(send_sems, recv_sems)
+    place = Place()
 
     def block_of(owner):
         return lax.rem(rank + count - owner, count)
 
     chain = Chain(
-        lambda owner, h: parts.at[owner, h],
-        lambda right, owner, h: slots.at[right, owner, h],
+        lambda owner, p: parts.at[owner, p],
+        lambda right, owner, p: slots.at[owner + right, p],
         chain_send,
         chain_recv,
-        2,
+        pieces,
     )
     near, far = chain.near, chain.far
-
-    greet("seq", "dp")
-    down[...] = lax.dot_general(
-        grad_ref[...], weight_ref[depth:, :], over_columns, preferred_element_type=f32
+    gathers, owns = [None], [None]
+    for source, target, view in scaled_pieces(scaled_ref, up_weight_ref, weight, own_cols)[2:]:
+        gathers.append(Gather(wires, place, source, target, view))
+        owns.append(
+            pltpu.make_async_copy(source, view(target, data_rank, None), local_sems.at[len(owns) - 1])
+        )
+    if pieces > 1:
+        gathers[1].first()
+    for copy in owns[1:]:
+        copy.start()
+
+    length = jnp.int32(0)
+    for p in range(devices):
+        length = length + jnp.where(owner_ref[p] == data_rank, lengths_ref[p], 0)
+
+    def head(h):
+        return pl.ds(pl.multiple_of(h * HD, HD), HD)
+
+    def head_step(h, carry):
+        keys = rms_scale(key_value_ref[:, head(h)], text_gain_ref[...]).astype(bf16)
+        values = key_value_ref[:, pl.ds(pl.multiple_of(depth + h * HD, HD), HD)].astype(bf16)
+        share = exp_scores(queries_ref[:, head(h)], keys)
+        position = lax.broadcasted_iota(jnp.int32, share.shape, 1)
+        share = jnp.where(position < length, share, 0.0)
+        denominator = denominator_ref[:, head(h)] + jnp.sum(share, -1, keepdims=True)
+        mixture = mixture_ref[:, head(h)] + jnp.dot(share.astype(bf16), values, preferred_element_type=f32)
+        attended[:, head(h)] = (mixture / denominator).astype(bf16)
+        return carry
+
+    lax.fori_loop(0, heads, head_step, 0)
+
+    def products(p, begin=True):
+        if p:
+            gathers[p].done()
+            owns[p].wait()
+        source = weight.at[p]
+        for step in range(count):
+            owner = chain.target(step, near)
+            block = attended[pl.ds(pl.multiple_of(block_of(owner) * rows, 16), rows), :]
+            if flat:
+                parts[owner, p] = jnp.dot(block, source[...], preferred_element_type=f32).astype(bf16)
+            else:
+                for d in range(devices):
+                    parts[owner, p, :, d * piece : (d + 1) * piece] = jnp.dot(
+                        block, source[d], preferred_element_type=f32
+                    ).astype(bf16)
+            if begin and step < count - 1:
+                chain.begin(step, (p,))
+
+    if flat:
+        down_total = lax.dot_general(grad_ref[...], up_weight_ref[...], over_columns, preferred_element_type=f32)
+    else:
+        down_total = jnp.zeros((rows, adapter), f32)
+        for d in range(devices):
+            down_total = down_total + lax.dot_general(
+                grad_ref[:, d * own_cols : (d + 1) * own_cols],
+                up_weight_ref[d],
+                over_columns,
+                preferred_element_type=f32,
+            )
+    down[...] = down_total.astype(bf16)
+    ups = lax.dot_general(
+        attended[...], dora_ref[...].astype(bf16), over_columns, preferred_element_type=f32
     ).astype(bf16)
+    for k in range(count):
+        up[k] = ups[k * rows : (k + 1) * rows]
     small = []
     for k, peer in peers("seq"):
         small.append(wires.send(down, down_slots.at[k - 1], "seq", peer))
-
-    length = jnp.int32(0)
-    for p in range(devices):
-        length = length + jnp.where(owner_ref[p] == data_rank, lengths_ref[p], 0)
-
-    def head(h):
-        return pl.ds(pl.multiple_of(h * HD, HD), HD)
-
-    def key_step(h, carry):
-        keys[:text, head(h)] = rms_scale(key_value_ref[:, head(h)], text_gain_ref[...]).astype(bf16)
-        for k in range(count):
-            start = text + k * rows
-            keys[start : start + rows, head(h)] = rms_scale(
-                image_ref[k, 1, :, head(h)].astype(f32), image_gain_ref[1:2, :]
-            ).astype(bf16)
-        return carry
-
-    lax.fori_loop(0, heads, key_step, 0)
-    values[:text, :] = key_value_ref[:, depth:].astype(bf16)
-    for k in range(count):
-        start = text + k * rows
-        values[start : start + rows, :] = image_ref[k, 2]
-    scale = 1.0 / math.sqrt(HD)
-
-    for step in range(count):
-        owner = chain.target(step, near)
-        block = block_of(owner)
-        block_slice = pl.ds(pl.multiple_of(block * rows, 16), rows)
-
-        def head_step(h, carry):
-            queries = rms_scale(
-                image_ref[block, 0, :, head(h)].astype(f32), image_gain_ref[0:1, :]
-            ).astype(bf16)
-            scores = lax.dot_general(queries, keys[:, head(h)], over_columns, preferred_element_type=f32) * scale
-            position = lax.broadcasted_iota(jnp.int32, scores.shape, 1)
-            weight = jnp.where((position < length) | (position >= text), jnp.exp(scores), 0.0)
-            denominator = jnp.sum(weight, -1, keepdims=True)
-            mixture = jnp.dot(weight.astype(bf16), values[:, head(h)], preferred_element_type=f32)
-            attended[block_slice, head(h)] = (mixture / denominator).astype(bf16)
-            return carry
-
-        lax.fori_loop(0, heads, head_step, 0)
-        for h in range(2):
-            columns = slice(h * half, (h + 1) * half)
-            parts[owner, h] = jnp.dot(
-                attended[block_slice, :], weight_ref[:depth, columns], preferred_element_type=f32
-            ).astype(bf16)
-        if step == 0:
-            chain.begin(0)
-
-    dora = dora_ref[...].astype(bf16)
-    ups = lax.dot_general(attended[...], dora, over_columns, preferred_element_type=f32).astype(bf16)
-    for k in range(count):
-        up[k] = ups[k * rows : (k + 1) * rows]
-    for k in range(1, count):
         before = lax.rem(rank + count - k, count)
         small.append(wires.send(up.at[k], up_slots.at[k - 1], "seq", before))
-    for step in range(1, count - 2):
-        chain.begin(step)
-    chain.forward(0, near)
+    products(0)
+    if pieces > 1:
+        gathers[1].second()
+    if pieces > 2:
+        gathers[2].first()
+
     for copy in small:
         copy.wait_recv()
     up_total = up[0].astype(f32)
@@ -733,6 +760,17 @@
     for k, peer in peers("dp"):
         first.append(wires.send(cols.at[peer], col_slots.at[k - 1], "dp", peer))
         first.append(wires.send(rows_all.at[peer], row_slots.at[k - 1], "dp", peer))
+
+    for p in range(1, pieces):
+        if p > 1:
+            gathers[p].second()
+            if p + 1 < pieces:
+                gathers[p + 1].first()
+        gathers[p].third()
+        products(p, p + 1 < pieces)
+        chain.forward(p - 1, near, (0,))
+    moves = [(p, step, side) for p in range(pieces) for step in range(count - 1) for side in (0, 1)]
+    moves = [m for m in moves if m not in [(0, p - 1, 0) for p in range(1, pieces)]]
     for copy in first:
         copy.wait_recv()
     col_total = cols[data_rank].astype(f32)
@@ -748,23 +786,22 @@
     for k, peer in peers("dp"):
         second.append(wires.send(row_stage, row_sums.at[data_rank], "dp", peer))
     row_sums[data_rank] = row_stage[...]
-    chain.begin(count - 2)
-    chain.forward(0, far)
-    for step in range(1, count - 1):
-        chain.forward(step, near)
-        chain.forward(step, far)
-
-    sums = []
-    for h in range(2):
-        chain.arrive(h)
-        columns = slice(h * half, (h + 1) * half)
-        total = chain.total(parts[rank, h], slots[1, rank, h], slots[0, rank, h])
-        image_out[:, columns] = total.astype(bf16)
-        sums.append(jnp.sum(grad_ref[:, columns].astype(f32) * total, 0, keepdims=True))
-    per_half = devices // 2
-    for d in range(devices):
-        start = (d % per_half) * own_cols
-        size[d] = sums[d // per_half][:, start : start + own_cols]
+    if pieces > 1:
+        for step in range(count - 1):
+            chain.begin(step, (pieces - 1,))
+    for p, step, side in moves:
+        chain.forward(step, far if side else near, (p,))
+
+    for p in range(pieces):
+        chain.arrive(p)
+        total = chain.total(parts[rank, p], slots[rank + 1, p], slots[rank, p])
+        for d in range(devices):
+            own = slice(d * own_cols + p * piece, d * own_cols + (p + 1) * piece)
+            block = total[:, d * piece : (d + 1) * piece]
+            image_out[:, own] = block.astype(bf16)
+            size[d, :, p * piece : (p + 1) * piece] = jnp.sum(
+                grad_ref[:, own].astype(f32) * block, 0, keepdims=True
+            )
     last = [wires.send(size.at[peer], size_slots.at[k - 1], "dp", peer) for k, peer in peers("dp")]
     for copy in second:
         copy.wait_recv()
@@ -790,57 +827,144 @@
     wires.drain()
 
 
-def back(owner, lengths, text_gain, image_gain, key_value, image, gathered, dora, grad, ratio, magnitude):
+def program_kernel(counts, *refs):
+    names = []
+    for n in counts:
+        names.append(refs[:n])
+        refs = refs[n:]
+    front_in, back_in, outs, shared, front_scratch, back_scratch = names
+    key_value, queries, mixture, denominator, own_scaled, weight, up_weight, ratio = shared
+    owner, down, magnitude = front_in[0], front_in[10], front_in[12]
+    waits = front_part(
+        *front_in, queries, mixture, denominator, key_value, own_scaled, weight, up_weight, ratio, *front_scratch
+    )
+    lengths, text_gain, grad = back_in
+    back_part(
+        owner, lengths, text_gain, key_value, queries, mixture, denominator,
+        own_scaled, weight, up_weight, down, grad, ratio, magnitude,
+        *outs, *back_scratch,
+    )
+    for wait in waits:
+        wait.drain()
+
+
+def program(
+    owner, enc, gain, w_in, w_out, final_gain, context, kv, image, proj, down, up, magnitude, scale, shift,
+    image_gain, lengths, text_gain, grad,
+):
     count, devices = lax.axis_size("seq"), lax.axis_size("dp")
-    rows, width = grad.shape
-    rank, depth = dora.shape
-    text = key_value.shape[0]
-    own_cols = ratio.shape[1]
+    bf16, f32 = jnp.bfloat16, jnp.float32
+    width_enc, hidden = w_in.shape[1:]
+    feat = width_enc // count
+    text = MAX_PROMPT
+    width = scale.shape[1]
+    text_rows = text // count
+    kinds, rows, _ = image.shape
+    head_width = width // count
+    depth, own_cols = proj.shape
+    rank = up.shape[0]
     block_rows = depth // devices
-    f32, bf16 = jnp.float32, jnp.bfloat16
-    others, data_others = count - 1, devices - 1
-    wires = 4 * others + 4 * data_others
+    pieces = pieces_of(own_cols)
+    piece = own_cols // pieces
+    others, data_others, pairs = count - 1, devices - 1, devices // 4
+    tile, out_tile = tile_of(hidden, 128), tile_of(feat, 512)
+    slots = 3
+    sum_chunks = feat // out_tile
+    per_gather = 6 * pairs - 3
+    front_wires = 4 * others + 4 * pairs + 4 * per_gather
+    back_wires = 4 * others + 4 * data_others + pieces * per_gather
+    any_ = pl.BlockSpec(memory_space=pl.ANY)
+    vmem, sems = pltpu.VMEM, pltpu.SemaphoreType.DMA
+    shared = [
+        vmem((text, kv.shape[1]), f32),
+        vmem((count * rows, head_width), bf16),
+        vmem((count * rows, head_width), f32),
+        vmem((count * rows, head_width), f32),
+        vmem((depth + rank, own_cols), bf16),
+        vmem((pieces,) + column_shape(devices, depth, piece), bf16),
+        vmem(column_shape(devices, rank, own_cols), bf16),
+        vmem((1, own_cols), f32),
+    ]
+    front_scratch = [
+        vmem((count, kinds, rows, head_width), bf16),
+        vmem((text, width_enc), bf16),
+        vmem((text, width_enc), bf16),
+        vmem((slots, width_enc, 2 * tile), bf16),
+        vmem((slots, hidden, out_tile), bf16),
+        vmem((text, hidden), bf16),
+        vmem((count, text, feat), bf16),
+        vmem((count + 1, text, feat), bf16),
+        vmem((text, feat), bf16),
+        vmem(column_shape(devices, context.shape[0], own_cols), bf16),
+        vmem((kv.shape[0] * devices, kv.shape[1]), bf16),
+        vmem((text, width), bf16),
+        vmem((count + 1, text_rows, width), bf16),
+        vmem((text_rows, width), bf16),
+        vmem((devices // 2 - 1, text_rows, width), bf16),
+        vmem((devices // 2, text_rows, width), bf16),
+        vmem((text, width), bf16),
+        vmem((depth, own_cols), f32),
+        vmem((1, own_cols), f32),
+        vmem((others, 1, own_cols), f32),
+        sems((slots * 2,)),
+        sems((slots,)),
+        sems((7,)),
+        sems((front_wires,)),
+        sems((front_wires,)),
+        sems((count * sum_chunks,)),
+        sems((count * 2 * sum_chunks,)),
+        sems((count * 2,)),
+        sems((count * 4,)),
+        sems((count * 2,)),
+        sems((count * 2,)),
+    ]
+    back_scratch = [
+        vmem((count * rows, head_width), bf16),
+        vmem((count, pieces, rows, devices * piece), bf16),
+        vmem((count + 1, pieces, rows, devices * piece), bf16),
+        vmem((rows, rank), bf16),
+        vmem((count, rows, rank), bf16),
+        vmem((others, rows, rank), bf16),
+        vmem((others, rows, rank), bf16),
+        vmem((devices, rank, own_cols), bf16),
+        vmem((data_others, rank, own_cols), bf16),
+        vmem((rank, own_cols), bf16),
+        vmem((others, rank, own_cols), bf16),
+        vmem((devices, rank, block_rows), bf16),
+        vmem((data_others, rank, block_rows), bf16),
+        vmem((rank, block_rows), bf16),
+        vmem((devices, rank, block_rows), bf16),
+        vmem((devices, 1, own_cols), f32),
+        vmem((data_others, 1, own_cols), f32),
+        vmem((1, own_cols), f32),
+        vmem((others, 1, own_cols), f32),
+        sems((pieces + 1,)),
+        sems((count * pieces,)),
+        sems((count * 2 * pieces,)),
+        sems((back_wires,)),
+        sems((back_wires,)),
+    ]
+    front_in = (
+        owner, enc, gain, w_in, w_out, final_gain, context, kv, image, proj, down, up, magnitude, scale, shift,
+        image_gain,
+    )
+    back_in = (lengths, text_gain, grad)
+    counts = (len(front_in), len(back_in), 4, len(shared), len(front_scratch), len(back_scratch))
     return pl.pallas_call(
-        back_kernel,
+        functools.partial(program_kernel, counts),
         out_shape=[
-            jax.ShapeDtypeStruct((rows, width), bf16),
+            jax.ShapeDtypeStruct(grad.shape, bf16),
             jax.ShapeDtypeStruct((rank, depth), f32),
             jax.ShapeDtypeStruct((rank, own_cols), f32),
             jax.ShapeDtypeStruct((1, own_cols), f32),
         ],
-        in_specs=[SMEM] * 2 + [VMEM] * 9,
+        in_specs=[SMEM, any_, VMEM, any_, any_, VMEM, any_, any_, any_] + [VMEM] * 7 + [SMEM, VMEM, VMEM],
         out_specs=[VMEM] * 4,
-        scratch_shapes=[
-            pltpu.VMEM((text + count * rows, depth), bf16),
-            pltpu.VMEM((text + count * rows, depth), bf16),
-            pltpu.VMEM((count * rows, depth), bf16),
-            pltpu.VMEM((count, 2, rows, width // 2), bf16),
-            pltpu.VMEM((2, count, 2, rows, width // 2), bf16),
-            pltpu.VMEM((rows, rank), bf16),
-            pltpu.VMEM((count, rows, rank), bf16),
-            pltpu.VMEM((others, rows, rank), bf16),
-            pltpu.VMEM((others, rows, rank), bf16),
-            pltpu.VMEM((devices, rank, own_cols), bf16),
-            pltpu.VMEM((data_others, rank, own_cols), bf16),
-            pltpu.VMEM((rank, own_cols), bf16),
-            pltpu.VMEM((others, rank, own_cols), bf16),
-            pltpu.VMEM((devices, rank, block_rows), bf16),
-            pltpu.VMEM((data_others, rank, block_rows), bf16),
-            pltpu.VMEM((rank, block_rows), bf16),
-            pltpu.VMEM((devices, rank, block_rows), bf16),
-            pltpu.VMEM((devices, 1, own_cols), f32),
-            pltpu.VMEM((data_others, 1, own_cols), f32),
-            pltpu.VMEM((1, own_cols), f32),
-            pltpu.VMEM((others, 1, own_cols), f32),
-            pltpu.SemaphoreType.DMA((count * 2,)),
-            pltpu.SemaphoreType.DMA((count * 4,)),
-            pltpu.SemaphoreType.DMA((wires,)),
-            pltpu.SemaphoreType.DMA((wires,)),
-        ],
+        scratch_shapes=shared + front_scratch + back_scratch,
         compiler_params=pltpu.CompilerParams(
-            collective_id=3, has_side_effects=True, vmem_limit_bytes=58 * 2**20
+            collective_id=1, has_side_effects=True, vmem_limit_bytes=63 * 2**20
         ),
-    )(owner, lengths, text_gain, image_gain, key_value, image, gathered, dora, grad, ratio, magnitude)
+    )(*front_in, *back_in)
 
 
 def on_device(
@@ -864,8 +988,7 @@
     magnitude,
     grad_out,
 ):
-    down = dora_a.T
-    image_all, key_value, gathered, ratio = front(
+    image_out, grad_a, grad_b, grad_magnitude = program(
         prompt_owner_sample,
         enc_states,
         t5_gain[None],
@@ -876,24 +999,15 @@
         kv_weight.reshape(kv_weight.shape[0], -1),
         jnp.transpose(image_query_key_value[0], (1, 0, 2)),
         proj_weight,
-        down,
+        dora_a.T,
         dora_b,
         magnitude[None],
         text_scale,
         text_shift,
-    )
-    image_out, grad_a, grad_b, grad_magnitude = back(
-        prompt_owner_sample,
+        image_qk_gain,
         lengths,
         text_key_gain[None],
-        image_qk_gain,
-        key_value,
-        image_all,
-        gathered,
-        down,
         grad_out[0],
-        ratio,
-        magnitude[None],
     )
     return (image_out[None], grad_a.T, grad_b, grad_magnitude[0])
 

time: 216 us -> 206 us (0.954)
  Pallas kernels: 205 us -> 195 us
    pallas_call x2 -> x1, Pallas kernels: 205 us -> 195 us  [program(): pl.pallas_call(functools.partial(program_kernel, counts), out_shape=[jax....]
where the time goes in v3:
time: 206 us
  Pallas kernels  195 us (95%)
  local copies, waits for them, and re-layouts  8.9 us (4%)
    pallas_call x1, Pallas kernels, program(): pl.pallas_call(functools.partial(program_kernel, counts), out_shape=[jax....  195 us
    unnamed x4, local copies, waits for them, and re-layouts  7.66 us

profile of v3, /device:TPU:0, one launch (start us, length us, event | category | flops | bytes accessed | tf_op | source)
XLA Modules:
  0.0 206.0 jit_solution(2362271393761381845)
XLA Ops:
  0.6 1.2 broadcast_in_dim.17.refs_12_
  1.9 2.4 %copy.23 = bf16[48,8,2,768]{3,1,2,0:T(8,128)(2,1)} copy(bf16[48,8,2,768]{3,2,1,0:T(2,128)(2,1)} %bitcast.14) | data formatting | bytes 2359296
  4.3 195.3 %shard_map.210 = (bf16[128,3072]{1,0:T(8,128)(2,1)}, f32[64,768]{1,0:T(8,128)}, f32[64,384]{1,0:T(8,128)}, f32[1,384]{1,0:T(1,128)}) custom-call(s32[8]{0:T(128)} %refs_0_.1, bf16[1,256,4096]{2,1,0:T(8,128)(2,1)} %refs_1_.1, f32[1,4096]{1,0:T(1,128)} %bitcast.19, bf16[2,4096,1280]{2,1,0:T(8,128)(2,1)} %refs_3_.1, bf16[1280,4096]{1,0:T(8,128)(2,1)} %refs_4_.1, ...), custom_call_target="tpu_custom_call" | custom-call | tf_op jit(solution)/shard_map/pallas_call | solution.py:953
  199.6 1.3 reduce
  200.8 2.1 %copy.27 = bf16[1,128,3072]{2,1,0:T(8,128)(2,1)} copy(bf16[1,128,3072]{2,1,0:T(8,128)(2,1)} %bitcast.15) | data formatting | bytes 1572864
  202.9 1.6 copy.28
  204.5 1.5 copy.29

commit v4 on v3

--- a/solution.py
+++ b/solution.py
@@ -544,13 +544,12 @@
                 ).astype(bf16)
         for step in range(count - 1):
             row_sums.begin(step, (c,))
-    kv_gather.second()
     for copy in square_copies:
         copy.wait_recv()
     total = squares[...]
     for k in range(1, count):
         total = total + square_slots[k - 1]
-    ratio = magnitude_ref[...] / jnp.sqrt(total + EPSILON)
+    ratio = magnitude_ref[...].reshape(1, own_cols) / jnp.sqrt(total + EPSILON)
     ratio_ref[...] = ratio
     for r in range(0, depth, 128):
         own_scaled[r : r + 128, :] = (direction[r : r + 128, :] * ratio).astype(bf16)
@@ -560,6 +559,8 @@
         for step in range(count - 1):
             row_sums.forward(step, row_sums.near, (c,))
             row_sums.forward(step, row_sums.far, (c,))
+        if c == 0:
+            kv_gather.second()
     for c in range(2):
         row_sums.arrive(c)
     stage[...] = row_sums.total(
@@ -734,12 +735,24 @@
         small.append(wires.send(down, down_slots.at[k - 1], "seq", peer))
         before = lax.rem(rank + count - k, count)
         small.append(wires.send(up.at[k], up_slots.at[k - 1], "seq", before))
+    def forwards(p):
+        for step in range(count - 1):
+            chain.forward(step, near, (p,))
+            chain.forward(step, far, (p,))
+
+    def prepare(p):
+        gathers[p].second()
+        if p + 1 < pieces:
+            gathers[p + 1].first()
+        gathers[p].third()
+        products(p, p + 1 < pieces)
+
     products(0)
     if pieces > 1:
-        gathers[1].second()
-    if pieces > 2:
-        gathers[2].first()
-
+        prepare(1)
+        forwards(0)
+    for p in range(2, pieces):
+        prepare(p)
     for copy in small:
         copy.wait_recv()
     up_total = up[0].astype(f32)
@@ -761,16 +774,8 @@
         first.append(wires.send(cols.at[peer], col_slots.at[k - 1], "dp", peer))
         first.append(wires.send(rows_all.at[peer], row_slots.at[k - 1], "dp", peer))
 
-    for p in range(1, pieces):
-        if p > 1:
-            gathers[p].second()
-            if p + 1 < pieces:
-                gathers[p + 1].first()
-        gathers[p].third()
-        products(p, p + 1 < pieces)
-        chain.forward(p - 1, near, (0,))
-    moves = [(p, step, side) for p in range(pieces) for step in range(count - 1) for side in (0, 1)]
-    moves = [m for m in moves if m not in [(0, p - 1, 0) for p in range(1, pieces)]]
+    for p in range(1, pieces - 1):
+        forwards(p)
     for copy in first:
         copy.wait_recv()
     col_total = cols[data_rank].astype(f32)
@@ -789,8 +794,7 @@
     if pieces > 1:
         for step in range(count - 1):
             chain.begin(step, (pieces - 1,))
-    for p, step, side in moves:
-        chain.forward(step, far if side else near, (p,))
+    forwards(pieces - 1)
 
     for p in range(pieces):
         chain.arrive(p)
@@ -822,7 +826,7 @@
         copy.wait_recv()
     for k, _ in peers("seq"):
         size_total = size_total + size_sums[k - 1]
-    size_out[...] = size_total / magnitude_ref[...]
+    size_out[...] = size_total / magnitude_ref[...].reshape(1, own_cols)
     chain.drain()
     wires.drain()
 
@@ -967,6 +971,19 @@
     )(*front_in, *back_in)
 
 
+def results_kernel(*refs):
+    half = len(refs) // 2
+    for source, target in zip(refs[:half], refs[half:]):
+        target[...] = source[...].reshape(target.shape)
+
+
+def results(*values):
+    shapes = [jax.ShapeDtypeStruct(v.shape if v.shape[0] > 1 else v.shape[1:], v.dtype) for v in values]
+    return pl.pallas_call(
+        results_kernel, out_shape=shapes, in_specs=[VMEM] * len(values), out_specs=[VMEM] * len(values)
+    )(*values)
+
+
 def on_device(
     enc_states,
     lengths,
@@ -988,7 +1005,7 @@
     magnitude,
     grad_out,
 ):
-    image_out, grad_a, grad_b, grad_magnitude = program(
+    outs = program(
         prompt_owner_sample,
         enc_states,
         t5_gain[None],
@@ -1001,7 +1018,7 @@
         proj_weight,
         dora_a.T,
         dora_b,
-        magnitude[None],
+        magnitude,
         text_scale,
         text_shift,
         image_qk_gain,
@@ -1009,7 +1026,8 @@
         text_key_gain[None],
         grad_out[0],
     )
-    return (image_out[None], grad_a.T, grad_b, grad_magnitude[0])
+    image_out, grad_a, grad_b, grad_magnitude = results(*outs)
+    return (image_out[None], grad_a.T, grad_b, grad_magnitude)
 
 
 def solution(mesh):

time: 206 us -> 202 us (0.981)
  local copies, waits for them, and re-layouts: 8.9 us -> 2.44 us
  Pallas kernels: 195 us -> 198 us
    unnamed x4 -> x1, local copies, waits for them, and re-layouts: 7.66 us -> 2.44 us
    pallas_call x0 -> x1, Pallas kernels: none -> 2.23 us  [results(): pl.pallas_call(results_kernel, out_shape=shapes, in_specs=[VMEM] * len(va...]
where the time goes in v4:
time: 202 us; the launch traced here: 201 us
  Pallas kernels  198 us (98%)
  local copies, waits for them, and re-layouts  2.44 us (1%)
    pallas_call x1, Pallas kernels, program(): pl.pallas_call(functools.partial(program_kernel, counts), out_shape=[jax....  196 us

profile of v4, /device:TPU:0, one launch (start us, length us, event | category | flops | bytes accessed | tf_op | source)
XLA Modules:
  0.0 201.3 jit_solution(1426858873713765215)
XLA Ops:
  0.6 2.4 %copy.23 = bf16[48,8,2,768]{3,1,2,0:T(8,128)(2,1)} copy(bf16[48,8,2,768]{3,2,1,0:T(2,128)(2,1)} %bitcast.14) | data formatting | bytes 2359296
  3.1 196.0 %shard_map.210 = (bf16[128,3072]{1,0:T(8,128)(2,1)}, f32[64,768]{1,0:T(8,128)}, f32[64,384]{1,0:T(8,128)}, f32[1,384]{1,0:T(1,128)}) custom-call(s32[8]{0:T(128)} %refs_0_.1, bf16[1,256,4096]{2,1,0:T(8,128)(2,1)} %refs_1_.1, f32[1,4096]{1,0:T(1,128)} %bitcast.17, bf16[2,4096,1280]{2,1,0:T(8,128)(2,1)} %refs_3_.1, bf16[1280,4096]{1,0:T(8,128)(2,1)} %refs_4_.1, ...), custom_call_target="tpu_custom_call" | custom-call | tf_op jit(solution)/shard_map/pallas_call | solution.py:957
  199.1 2.2 %shard_map.211 = (bf16[128,3072]{1,0:T(8,128)(2,1)}, f32[64,768]{1,0:T(8,128)}, f32[64,384]{1,0:T(8,128)}, f32[384]{0:T(512)}) custom-call(bf16[128,3072]{1,0:T(8,128)(2,1)} %get-tuple-element.12.refs_0_, f32[64,768]{1,0:T(8,128)} %get-tuple-element.13.refs_1_, f32[64,384]{1,0:T(8,128)} %get-tuple-element.14.refs_2_, f32[1,384]{1,0:T(1,128)} %get-tuple-element.15.refs_3_), custom_call_target="tpu_custom_call" | custom-call | tf_op jit(solution)/shard_map/pallas_call | solution.py:982

commit v5 on v4

--- a/solution.py
+++ b/solution.py
@@ -518,6 +518,7 @@
     context_gather.done()
     if late > 1:
         image(late, 1)
+        image(late, 2)
 
     def block_of(index):
         return pl.ds(pl.multiple_of(index * rows, 16), rows)
@@ -559,8 +560,6 @@
         for step in range(count - 1):
             row_sums.forward(step, row_sums.near, (c,))
             row_sums.forward(step, row_sums.far, (c,))
-        if c == 0:
-            kv_gather.second()
     for c in range(2):
         row_sums.arrive(c)
     stage[...] = row_sums.total(
@@ -576,6 +575,7 @@
     ]
     shared = [wires.send(stage, sibling_prompts.at[0], "dp", sibling)]
     images((1, 2))
+    kv_gather.second()
     for gather, copy in zip(scaled_gathers, scaled_locals):
         gather.first()
         copy.start()
@@ -600,8 +600,6 @@
     spread = jnp.mean((routed - centre) * (routed - centre), -1, keepdims=True)
     layer_normed = (routed - centre) * lax.rsqrt(spread + EPSILON)
     text_all[block_of(rank), :] = ((1.0 + scale_ref[...]) * layer_normed + shift_ref[...]).astype(bf16)
-    if late > 1:
-        image(late, 2)
     texts = Relay(lambda owner: text_all.at[block_of(owner)], text_send, text_recv)
     texts.begin()
     for k in [k for k in range(2, count) if k != late] + [late] * (late > 1):

time: 202 us -> 196 us (0.970)
  Pallas kernels: 198 us -> 193 us
    pallas_call x1, Pallas kernels: 196 us -> 191 us  [program(): pl.pallas_call(functools.partial(program_kernel, counts), out_shape=[jax....]
where the time goes in v5:
time: 196 us
  Pallas kernels  193 us (98%)
  local copies, waits for them, and re-layouts  2.44 us (1%)
    pallas_call x1, Pallas kernels, program(): pl.pallas_call(functools.partial(program_kernel, counts), out_shape=[jax....  191 us

profile of v5, /device:TPU:0, one launch (start us, length us, event | category | flops | bytes accessed | tf_op | source)
XLA Modules:
  0.0 195.9 jit_solution(12179819636865673665)
XLA Ops:
  0.6 2.4 %copy.23 = bf16[48,8,2,768]{3,1,2,0:T(8,128)(2,1)} copy(bf16[48,8,2,768]{3,2,1,0:T(2,128)(2,1)} %bitcast.14) | data formatting | bytes 2359296
  3.1 190.6 %shard_map.210 = (bf16[128,3072]{1,0:T(8,128)(2,1)}, f32[64,768]{1,0:T(8,128)}, f32[64,384]{1,0:T(8,128)}, f32[1,384]{1,0:T(1,128)}) custom-call(s32[8]{0:T(128)} %refs_0_.1, bf16[1,256,4096]{2,1,0:T(8,128)(2,1)} %refs_1_.1, f32[1,4096]{1,0:T(1,128)} %bitcast.17, bf16[2,4096,1280]{2,1,0:T(8,128)(2,1)} %refs_3_.1, bf16[1280,4096]{1,0:T(8,128)(2,1)} %refs_4_.1, ...), custom_call_target="tpu_custom_call" | custom-call | tf_op jit(solution)/shard_map/pallas_call | solution.py:955
  193.7 2.2 %shard_map.211 = (bf16[128,3072]{1,0:T(8,128)(2,1)}, f32[64,768]{1,0:T(8,128)}, f32[64,384]{1,0:T(8,128)}, f32[384]{0:T(512)}) custom-call(bf16[128,3072]{1,0:T(8,128)(2,1)} %get-tuple-element.12.refs_0_, f32[64,768]{1,0:T(8,128)} %get-tuple-element.13.refs_1_, f32[64,384]{1,0:T(8,128)} %get-tuple-element.14.refs_2_, f32[1,384]{1,0:T(1,128)} %get-tuple-element.15.refs_3_), custom_call_target="tpu_custom_call" | custom-call | tf_op jit(solution)/shard_map/pallas_call | solution.py:980
